TPU v7x, 256 devices: a whole 4x4x8 slice. The times are simulated.
256 devices in a mesh: seq: 16 (over y, x_hi, core), head: 16 (over x_lo, z).
Axes of the slice: x: 4 (x_hi: 2, x_lo: 2; x = x_hi * 2 + x_lo), y: 4, z: 8, core: 2. Of those that a mesh axis runs over, the one named last changes fastest.
Arguments:
- latent_cache: bfloat16 [2, 32768, 576], P(None, 'seq'), may hold values from -8 to 8
- draft_latent: bfloat16 [2, 64, 576], P(None, 'seq'), may hold values from -9 to 9
- query_nope: bfloat16 [2, 64, 128, 128], P(None, None, 'head'), may hold values from -6 to 6
- query_rope: bfloat16 [2, 64, 128, 64], P(None, None, 'head'), may hold values from -8 to 8
- parents: int32 [2, 64], replicated, may hold values from -1 to 62, as said below
- lengths: int32 [2], replicated, may hold values from 16384 to 32768
- key_weight: bfloat16 [128, 128, 512], P('head'), may hold values from -0.25 to 0.25
- value_weight: bfloat16 [128, 512, 128], P('head'), may hold values from -0.25 to 0.25
- out_weight: bfloat16 [16384, 7168], P('head', 'seq'), may hold values from -0.046875 to 0.046875
- residual: bfloat16 [2, 64, 7168], P(None, None, 'seq'), may hold values from -40 to 40
- norm_gain: bfloat16 [7168], P('seq'), may hold values from 0.5 to 1.5
- vocab_weight: bfloat16 [7168, 65536], P('seq', 'head'), may hold values from -0.21875 to 0.21875
Outputs:
- logits: bfloat16 [2, 64, 65536], P(None, None, ('head', 'seq'))
Inputs may be any that keep to these rules, and one draw needn't show every extreme that they name: `parents`: token 0 is the root of each tree with parent -1; every other token's parent is an earlier token; the last token's parent is the token just before it.
All inputs are finite; a program needn't handle non-finite values.
Results may differ from a plain program's by a relative error of at most 0.02.
Values may be sent and summed in bfloat16 or wider, within the bound.
A program may use at most 64 MiB of HBM per device.

v0:
```python
import math

import jax
import jax.numpy as jnp
from jax import lax
from jax.sharding import PartitionSpec as P

D = 7168


NEGATIVE = -1e30
EPSILON = 1e-06


def sent_to_all(array, axis):
    copies = jnp.broadcast_to(array, (lax.axis_size(axis), *array.shape))
    return lax.all_to_all(copies, axis, split_axis=0, concat_axis=0, tiled=True)


def over_copies(array, axis):
    return sent_to_all(array, axis).max(axis=0)


def split_up(array, dim, devices):
    before, after = (array.shape[:dim], array.shape[dim + 1 :])
    return jnp.moveaxis(array.reshape(*before, devices, -1, *after), dim, 0)


def sent_and_summed(array, axis, dim):
    devices = lax.axis_size(axis)
    pieces = lax.all_to_all(split_up(array, dim, devices), axis, 0, 0, tiled=True)
    return jnp.sum(pieces.astype(jnp.float32), axis=0)


def in_one_piece(arrays, axis, dim, along):
    widths = [math.prod(a.shape[along:]) for a in arrays]
    both = jnp.concatenate(
        [a.reshape(*a.shape[:along], w) for a, w in zip(arrays, widths)], axis=along
    )
    filled = sent_and_summed(both, axis, dim)
    pieces = jnp.split(filled, [sum(widths[:k]) for k in range(1, len(widths))], axis=along)
    return tuple(
        (b.reshape(*filled.shape[:along], *a.shape[along:]) for a, b in zip(arrays, pieces))
    )


def joined_along(pieces, dim):
    shape = list(pieces.shape[1:])
    shape[dim] *= pieces.shape[0]
    return jnp.moveaxis(pieces, 0, dim).reshape(shape)


def gathered_copies(array, axis, dim):
    pieces = sent_to_all(array, axis)
    return joined_along(pieces, dim)


def filled_up(lines, devices):
    spare = -len(lines) % devices
    return jnp.pad(lines, [(0, spare)] + [(0, 0)] * (lines.ndim - 1))


def sum_by_parts(array, axes):
    lines = array.reshape(-1, array.shape[-1])
    own = sent_and_summed(filled_up(lines, lax.axis_size(axes)), axes, 0)
    whole = gathered_copies(own.astype(jnp.bfloat16), axes, 0)
    return whole[: len(lines)].reshape(array.shape).astype(jnp.float32)


def over_copies_2(array, axis):
    return sent_to_all(array, axis).sum(axis=0)


def ancestry_of(parents):
    token_count = parents.shape[1]
    indices = jnp.arange(token_count, dtype=jnp.int32)
    linked = (parents[:, :, None] == indices[None, None, :]) | (
        indices[:, None] == indices[None, :]
    )[None]
    reachable = linked.astype(jnp.float32)
    for repeat in range(max(1, (token_count - 1).bit_length())):
        product = jnp.einsum("bij,bjk->bik", reachable, reachable, precision=lax.Precision.HIGHEST)
        reachable = jnp.where(product > 0.5, 1.0, 0.0).astype(jnp.float32)
    return reachable


def per_device(
    latent_cache,
    draft_latent,
    query_nope,
    query_rope,
    parents,
    lengths,
    key_weight,
    value_weight,
    out_weight,
    residual,
    norm_gain,
    vocab_weight,
):
    requests, cache_local, width = latent_cache.shape
    latent = value_weight.shape[1]
    heads_local = key_weight.shape[0]
    drafted = query_nope.shape[1]
    draft_local = draft_latent.shape[1]
    scaling = 1.0 / math.sqrt(query_nope.shape[3] + query_rope.shape[3])
    seat = lax.axis_index("seq")
    absorbed = jnp.einsum(
        "bthn,hnl->bthl", query_nope, key_weight, preferred_element_type=jnp.float32
    ).astype(jnp.bfloat16)
    queries = jnp.concatenate([absorbed, query_rope], axis=-1)
    ancestry = ancestry_of(parents)
    own_tree = lax.dynamic_slice_in_dim(ancestry, seat * draft_local, draft_local, 2)
    positions = seat * cache_local + jnp.arange(cache_local, dtype=jnp.int32)
    live = positions[None, :] < lengths[:, None]
    cache_values = latent_cache[:, :, :latent]
    draft_values = draft_latent[:, :, :latent]
    row_count = drafted * heads_local
    block = queries.reshape(requests, row_count, width)
    tree_block = own_tree
    tree_block = jnp.broadcast_to(
        tree_block[:, :, None, :], (requests, drafted, heads_local, draft_local)
    )
    tree_block = tree_block.reshape(requests, row_count, draft_local)
    cache_scores = (
        jnp.einsum("brc,bkc->brk", block, latent_cache, preferred_element_type=jnp.float32)
        * scaling
    )
    cache_scores = jnp.where(live[:, None, :], cache_scores, NEGATIVE)
    draft_scores = (
        jnp.einsum("brc,bkc->brk", block, draft_latent, preferred_element_type=jnp.float32)
        * scaling
    )
    draft_scores = jnp.where(tree_block > 0.5, draft_scores, NEGATIVE)
    cache_scores, draft_scores, tree_block = (cache_scores, draft_scores, tree_block)
    local_max = jnp.maximum(jnp.max(cache_scores, -1), jnp.max(draft_scores, -1))
    row_max = over_copies(local_max, "seq")
    cache_weights = jnp.where(live[:, None, :], jnp.exp(cache_scores - row_max[..., None]), 0.0)
    draft_weights = jnp.where(tree_block > 0.5, jnp.exp(draft_scores - row_max[..., None]), 0.0)
    total = jnp.sum(cache_weights, -1) + jnp.sum(draft_weights, -1)
    mixed = jnp.einsum(
        "brk,bkl->brl",
        cache_weights.astype(jnp.bfloat16),
        cache_values,
        preferred_element_type=jnp.float32,
    )
    mixed = mixed + jnp.einsum(
        "brk,bkl->brl",
        draft_weights.astype(jnp.bfloat16),
        draft_values,
        preferred_element_type=jnp.float32,
    )
    total, mixed = (total, mixed)
    own_total, own_mixed = in_one_piece(
        (total.astype(jnp.bfloat16), mixed.astype(jnp.bfloat16)), "seq", 1, 2
    )
    latent_out = (own_mixed / own_total[..., None]).astype(jnp.bfloat16)
    latent_out = latent_out.reshape(requests, draft_local, heads_local, latent)
    per_head = jnp.einsum(
        "bthl,hlv->bthv", latent_out, value_weight, preferred_element_type=jnp.float32
    ).astype(jnp.bfloat16)
    head_values = per_head.reshape(requests, draft_local, heads_local * value_weight.shape[2])
    attention = jnp.dot(
        gathered_copies(head_values, "seq", 1), out_weight, preferred_element_type=jnp.float32
    )
    attention = sum_by_parts(attention.astype(jnp.bfloat16), "head")
    hidden = residual.astype(jnp.float32) + attention
    squares = over_copies_2(jnp.sum(hidden * hidden, -1), "seq")
    normed = (
        hidden * lax.rsqrt(squares / D + EPSILON)[..., None] * norm_gain.astype(jnp.float32)
    ).astype(jnp.bfloat16)
    partial_logits = jnp.dot(normed, vocab_weight, preferred_element_type=jnp.float32)
    return sent_and_summed(partial_logits.astype(jnp.bfloat16), "seq", 2).astype(jnp.bfloat16)


def solution(mesh):
    in_specs = (
        P(None, "seq", None),
        P(None, "seq", None),
        P(None, None, "head", None),
        P(None, None, "head", None),
        P(),
        P(),
        P("head", None, None),
        P("head", None, None),
        P("head", "seq"),
        P(None, None, "seq"),
        P("seq"),
        P("seq", "head"),
    )
    out_specs = P(None, None, ("head", "seq"))
    return jax.shard_map(
        per_device, mesh=mesh, in_specs=in_specs, out_specs=out_specs, check_vma=False
    )
```

profile of v0, /device:TPU:1, one launch (start us, length us, event | category | flops | bytes accessed | tf_op | source)
XLA Modules:
  0.0 143.4 jit_solution(2327715782805970922)
XLA Ops:
  0.0 0.0 copy-start
  0.0 1.1 fusion.40
  1.1 0.2 fusion.41
  1.4 0.2 fusion.42
  1.6 0.2 fusion.43
  1.9 0.2 fusion.44
  2.1 0.2 fusion.59
  2.4 0.1 broadcast_in_dim.78
  2.5 0.2 gt.33
  2.7 1.0 copy.87
  3.7 0.0 copy-start.7
  3.7 1.0 copy.88
  4.7 0.0 copy-done
  4.7 0.4 fusion.101
  5.1 0.0 copy-start.5
  5.1 0.0 copy-start.8
  5.2 0.1 convert_bitcast_fusion
  5.3 0.0 copy-done.7
  5.3 0.1 broadcast_compare_fusion
  5.4 0.1 pad_maximum_fusion
  5.5 0.3 copy-done.5
  5.8 0.8 fusion.100
  6.7 0.8 copy-done.8
  7.5 6.0 %fusion = (f32[2,512]{1,0:T(2,128)S(1)}, f32[2,512,2048]{2,1,0:T(8,128)}) fusion(pred[2,2048]{1,0:T(4,128)(4,1)S(1)} %broadcast_compare_fusion, bf16[2,2048,576]{1,2,0:T(8,128)(2,1)S(1)} %copy-done.8, bf16[2,64,8,576]{3,1,0,2:T(8,128)(2,1)S(1)} %pad_maximum_fusion), kind=kOutput, calls=%fused_computation.2 | convolution fusion | flops 2422209536 | bytes 14295040 | tf_op jit(solution)/shard_map/brc,bkc->brk/dot_general | solution.py:126
  13.6 15.6 %all_to_all.35 = f32[16,2,512]{2,1,0:T(2,128)S(1)} all-to-all(f32[16,2,512]{2,1,0:T(2,128)S(1)} %broadcast_in_dim.80), channel_id=1, replica_groups=mesh['seq'=16,'head'=16] {'seq'}, dimensions={0} | all-to-all | bytes 131072 | tf_op jit(solution)/shard_map/all_to_all | solution.py:17
  29.2 0.0 copy-start.1
  29.2 5.1 %fusion.2 = f32[2,512]{1,0:T(2,128)S(1)} fusion(f32[2,512,2048]{2,1,0:T(8,128)} %get-tuple-element.6, f32[2,512]{1,0:T(2,128)S(1)} %reduce_max.29, pred[2,2048]{1,0:T(4,128)(4,1)S(1)} %broadcast_compare_fusion), kind=kLoop, calls=%fused_computation.4 | loop fusion | flops 10484736 | bytes 8400896 | tf_op jit(solution)/shard_map/reduce_sum | solution.py:140
  34.3 0.7 copy-done.1
  35.0 4.3 %fusion.3 = f32[2,512,512]{2,1,0:T(8,128)S(1)} fusion(f32[2,512,2048]{2,1,0:T(8,128)S(1)} %copy-done.1, bf16[2,2048,576]{1,2,0:T(8,128)(2,1)} %param.12, f32[2,512]{1,0:T(2,128)S(1)} %reduce_max.29, pred[2,2048]{1,0:T(4,128)(4,1)S(1)} %broadcast_compare_fusion), kind=kOutput, calls=%fused_computation.6 | convolution fusion | flops 2157969408 | bytes 14688256 | tf_op jit(solution)/shard_map/brk,bkl->brl/dot_general | solution.py:141
  39.4 0.5 add_convert_fusion
  39.9 0.0 copy-start.2
  39.9 0.1 convert_element_type.71
  40.0 0.3 copy.108
  40.3 0.7 maximum_bitcast_fusion
  41.0 0.0 copy-start.3
  41.0 23.0 %all_to_all.36 = bf16[16,2,32,513]{3,2,1,0:T(8,128)(2,1)S(1)} all-to-all(bf16[16,2,32,513]{3,2,1,0:T(8,128)(2,1)S(1)} %maximum_bitcast_fusion), channel_id=1, replica_groups=mesh['seq'=16,'head'=16] {'seq'}, dimensions={0} | all-to-all | bytes 2101248 | tf_op jit(solution)/shard_map/all_to_all | solution.py:31
  64.0 0.0 copy-start.4
  64.0 0.0 copy-start.6
  64.0 0.2 convert_reduce_fusion
  64.2 0.1 slice_reduce_fusion
  64.3 0.1 fusion.65
  64.4 0.0 copy-done.2
  64.4 0.3 fusion.33
  64.7 0.1 broadcast_in_dim.83
  64.8 12.2 %all_to_all.37 = bf16[16,2,4,1024]{3,2,1,0:T(4,128)(2,1)S(1)} all-to-all(bf16[16,2,4,1024]{3,2,1,0:T(4,128)(2,1)S(1)} %broadcast_in_dim.83), channel_id=1, replica_groups=mesh['seq'=16,'head'=16] {'seq'}, dimensions={0} | all-to-all | bytes 524288 | tf_op jit(solution)/shard_map/all_to_all | solution.py:17
  77.0 0.1 copy.112
  77.1 0.1 reshape.104
  77.1 0.0 copy-done.3
  77.1 0.4 convolution_convert_fusion.1
  77.6 15.6 %all_to_all.38 = bf16[16,8,448]{2,1,0:T(8,128)(2,1)S(1)} all-to-all(bf16[16,8,448]{2,1,0:T(8,128)(2,1)S(1)} %bitcast.71), channel_id=1, replica_groups=mesh['seq'=16,'head'=16] {'head'}, dimensions={0} | all-to-all | bytes 229376 | tf_op jit(solution)/shard_map/all_to_all | solution.py:31
  93.3 10.4 %all_to_all.39 = bf16[16,8,448]{2,1,0:T(8,128)(2,1)S(1)} all-to-all(bf16[16,8,448]{2,1,0:T(8,128)(2,1)S(1)} %broadcast_in_dim.84), channel_id=1, replica_groups=mesh['seq'=16,'head'=16] {'head'}, dimensions={0} | all-to-all | bytes 229376 | tf_op jit(solution)/shard_map/all_to_all | solution.py:17
  103.7 0.0 copy-done.4
  103.7 0.1 multiply_reduce_fusion
  103.8 0.7 reshape.114
  104.5 6.9 %all-to-all-start.5 = ((f32[16,1,128]{2,1,0:T(1,128)}), f32[16,1,128]{2,1,0:T(1,128)S(1)}, u32[]{:S(2)}, u32[]{:S(2)}) async-start(f32[16,1,128]{2,1,0:T(1,128)} %reshape.114), calls=%async_computation.5 | async-start | bytes 16384 | tf_op jit(solution)/shard_map/all_to_all | solution.py:17
  111.4 0.0 copy-done.6
  111.4 6.9 %all-to-all-done.5 = f32[16,1,128]{2,1,0:T(1,128)S(1)} async-done(((f32[16,1,128]{2,1,0:T(1,128)}), f32[16,1,128]{2,1,0:T(1,128)S(1)}, u32[]{:S(2)}, u32[]{:S(2)}) %all-to-all-start.5) | async-done | bytes 8224 | tf_op jit(solution)/shard_map/all_to_all | solution.py:17
  118.3 0.5 broadcast.77
  118.8 0.7 reduce.14
  119.5 0.1 reshape.115
  119.6 2.8 %convolution_convert_fusion = bf16[2,64,4096]{2,1,0:T(8,128)(2,1)S(1)} fusion(bf16[448,4096]{1,0:T(8,128)(2,1)} %param.23, bf16[2,64,448]{2,1,0:T(8,128)(2,1)S(1)} %bitcast.68, bf16[2,64,448]{2,1,0:T(8,128)(2,1)S(1)} %copy-done.4, f32[448]{0:T(512)S(1)} %convert_element_type.82, f32[2,64]{1,0:T(2,128)S(1)} %add_rsqrt_fusion), kind=kOutput, calls=%fused_computation.5 | convolution fusion | flops 470630400 | bytes 4950272 | tf_op jit(solution)/shard_map/dot_general | solution.py:172
  122.4 0.1 copy.159
  122.6 20.1 %all_to_all.40 = bf16[16,2,64,256]{3,2,1,0:T(8,128)(2,1)S(1)} all-to-all(bf16[16,2,64,256]{3,2,1,0:T(8,128)(2,1)S(1)} %bitcast.66), channel_id=1, replica_groups=mesh['seq'=16,'head'=16] {'seq'}, dimensions={0} | all-to-all | bytes 2097152 | tf_op jit(solution)/shard_map/all_to_all | solution.py:31
  142.7 0.8 reduce_sum.75
  (20 shorter events, 0.4 us)
Async XLA Ops:
  0.0 4.7 %copy-start = (bf16[8,128,512]{2,1,0:T(8,128)(2,1)S(1)}, bf16[8,128,512]{2,1,0:T(8,128)(2,1)}, u32[]{:S(2)}) copy-start(bf16[8,128,512]{2,1,0:T(8,128)(2,1)} %param.18) | copy-start | bytes 3145732
  3.7 1.6 %copy-start.7 = (s32[2]{0:T(128)S(1)}, s32[2]{0:T(128)}, u32[]{:S(2)}) copy-start(s32[2]{0:T(128)} %param.17) | copy-start | bytes 28
  5.1 0.7 copy-start.5
  5.1 2.3 %copy-start.8 = (bf16[2,2048,576]{1,2,0:T(8,128)(2,1)S(1)}, bf16[2,2048,576]{1,2,0:T(8,128)(2,1)}, u32[]{:S(2)}) copy-start(bf16[2,2048,576]{1,2,0:T(8,128)(2,1)} %param.12) | copy-start | bytes 14155780
  29.2 5.8 %copy-start.1 = (f32[2,512,2048]{2,1,0:T(8,128)S(1)}, f32[2,512,2048]{2,1,0:T(8,128)}, u32[]{:S(2)}) copy-start(f32[2,512,2048]{2,1,0:T(8,128)} %get-tuple-element.6) | copy-start | bytes 25165828
  39.9 24.6 %copy-start.2 = (bf16[8,512,128]{2,1,0:T(8,128)(2,1)S(1)}, bf16[8,512,128]{2,1,0:T(8,128)(2,1)}, u32[]{:S(2)}) copy-start(bf16[8,512,128]{2,1,0:T(8,128)(2,1)} %param.19) | copy-start | bytes 3145732
  41.0 36.1 %copy-start.3 = (bf16[1024,448]{0,1:T(8,128)(2,1)S(1)}, bf16[1024,448]{0,1:T(8,128)(2,1)}, u32[]{:S(2)}) copy-start(bf16[1024,448]{0,1:T(8,128)(2,1)} %param.20) | copy-start | bytes 2752516
  64.0 39.7 %copy-start.4 = (bf16[2,64,448]{2,1,0:T(8,128)(2,1)S(1)}, bf16[2,64,448]{2,1,0:T(8,128)(2,1)}, u32[]{:S(2)}) copy-start(bf16[2,64,448]{2,1,0:T(8,128)(2,1)} %param.21) | copy-start | bytes 344068
  64.0 47.4 %copy-start.6 = (bf16[448]{0:T(512)(128)(2,1)S(1)}, bf16[448]{0:T(512)(128)(2,1)}, u32[]{:S(2)}) copy-start(bf16[448]{0:T(512)(128)(2,1)} %param.22) | copy-start | bytes 2692
  104.5 13.8 %all-to-all-start.5 = ((f32[16,1,128]{2,1,0:T(1,128)}), f32[16,1,128]{2,1,0:T(1,128)S(1)}, u32[]{:S(2)}, u32[]{:S(2)}) async-start(f32[16,1,128]{2,1,0:T(1,128)} %reshape.114), calls=%async_computation.5 | async-start | bytes 16384 | tf_op jit(solution)/shard_map/all_to_all | solution.py:17
where the time goes:
time: 144 us; the launch traced here: 143 us
  blocking collectives  96.8 us (67%)
  matrix products  17.7 us (12%)
  other arithmetic  8.42 us (6%)
  starting transfers between devices  6.92 us (5%)
  waiting for transfers between devices  6.9 us (5%)
  local copies, waits for them, and re-layouts  6.36 us (4%)
    all_to_all x3, blocking collectives, sent_and_summed(): lax.all_to_all(split_up(array, dim, devices), axis, 0, 0, tiled=True)  58.7 us
    all_to_all x3, blocking collectives, sent_to_all(): return lax.all_to_all(copies, axis, split_axis=0, concat_axis=0, tiled=True)  38.1 us
    all_to_all x1, starting transfers between devices, sent_to_all(): return lax.all_to_all(copies, axis, split_axis=0, concat_axis=0, tiled=True)  6.92 us
    all_to_all x1, waiting for transfers between devices, sent_to_all(): return lax.all_to_all(copies, axis, split_axis=0, concat_axis=0, tiled=True)  6.9 us
    dot_general x1, matrix products, per_device(): jnp.einsum('brc,bkc->brk', block, latent_cache, preferred_element_type=jn...  6.03 us
    reduce_sum x2, other arithmetic, per_device(): total = jnp.sum(cache_weights, -1) + jnp.sum(draft_weights, -1)  5.18 us
    unnamed x22, local copies, waits for them, and re-layouts  4.62 us
    dot_general x1, matrix products, per_device(): jnp.einsum('brk,bkl->brl', cache_weights.astype(jnp.bfloat16), cache_valu...  4.33 us
  transfers between devices with their start and end apart: 1, of which 1 were waited for; matrix products, arithmetic and copies ran while one was open for 0% of the time, Pallas kernels for 0%

commit v1 on v0

v1 whole, which is shorter than its diff:
```python
import functools
import math

import jax
import jax.numpy as jnp
from jax import lax
from jax.experimental import pallas as pl
from jax.experimental.pallas import tpu as pltpu
from jax.sharding import PartitionSpec as P

MESH = pl.DeviceIdType.MESH
NEGATIVE = -1e30
EPSILON = 1e-06
F32 = jnp.float32
BF16 = jnp.bfloat16

CHIP_STEPS = [(2, 1), (1, 1), (3, 1), (2, 0), (0, 1), (1, 0), (3, 0)]
SEQ_STEPS = [(dy, dx, dk) for dy, dx in CHIP_STEPS for dk in (0, 1)] + [(0, 0, 1)]
REQUESTS, DRAFT, HEADS, LATENT, ROPE, WIDTH = 2, 64, 8, 512, 64, 576
TOKENS = REQUESTS * DRAFT
KEYS, PADDED = 2048, 2176
BLOCK = 256


def nt_dot(a, b):
    return lax.dot_general(a, b, (((1,), (1,)), ((), ())), preferred_element_type=F32)


def dot(a, b):
    return jnp.dot(a, b, preferred_element_type=F32)


def kernel(
    model_width,
    lengths,
    parents_hbm,
    cache_hbm,
    draft_hbm,
    nope_hbm,
    rope_hbm,
    key_hbm,
    value_hbm,
    out_hbm,
    residual_hbm,
    gain_hbm,
    vocab_hbm,
    logits,
    parents,
    kbuf,
    nope,
    rope,
    key_weight,
    value_weight,
    out_weight,
    residual,
    gain,
    vocab,
    nope32,
    rope32,
    qbuf,
    pbuf,
    o_send,
    o_recv,
    ml_send,
    ml_recv,
    g_send,
    g_full,
    a_send,
    a_recv,
    b_send,
    b_full,
    s_send,
    s_recv,
    p_send,
    p_recv,
    l_send,
    l_recv,
    load_sems,
    vocab_sems,
    local_sems,
    o_sems,
    ml_sems,
    g_sems,
    a_sems,
    b_sems,
    s_sems,
    p_sems,
    l_sems,
):
    seat = lax.axis_index("seq")
    mine = lax.axis_index("head")
    y = lax.div(seat, 4)
    xh = lax.rem(lax.div(seat, 2), 2)
    core = lax.rem(seat, 2)
    chip = lax.div(seat, 2)

    def seat_at(dy, dx, dk):
        return lax.rem(y + dy, 4) * 4 + lax.rem(xh + dx, 2) * 2 + lax.rem(core + dk, 2)

    seq_peers = [seat_at(*step) for step in SEQ_STEPS]
    head_peers = [lax.rem(mine + j, 16) for j in range(1, 16)]

    barrier = pltpu.get_barrier_semaphore()
    for peer in seq_peers:
        pl.semaphore_signal(barrier, inc=1, device_id={"seq": peer}, device_id_type=MESH)
    for peer in head_peers:
        pl.semaphore_signal(barrier, inc=1, device_id={"head": peer}, device_id_type=MESH)

    loads = []

    def load(src, dst):
        copy = pltpu.make_async_copy(src, dst, load_sems.at[len(loads)])
        loads.append(copy)
        copy.start()
        return copy

    got_nope = load(nope_hbm, nope)
    got_rope = load(rope_hbm, rope)
    got_key = load(key_hbm, key_weight)
    got_parents = load(parents_hbm, parents)
    got_draft = [load(draft_hbm, kbuf.at[b, pl.ds(KEYS, 16), :]) for b in range(REQUESTS)]
    got_cache = [load(cache_hbm.at[b], kbuf.at[b, pl.ds(0, KEYS), :]) for b in range(REQUESTS)]
    got_value = load(value_hbm, value_weight)
    got_out = load(out_hbm, out_weight)
    got_residual = load(residual_hbm, residual)
    got_gain = load(gain_hbm, gain)

    vocab_order = []
    for half in (1, 0):
        for dy, dx in CHIP_STEPS + [(0, 0)]:
            vocab_order.append(seat_at(dy, dx, half))
    got_vocab = []
    for slot, owner in enumerate(vocab_order):
        columns = pl.ds(pl.multiple_of(owner * 256, 256), 256)
        copy = pltpu.make_async_copy(
            vocab_hbm.at[:, columns], vocab.at[slot], vocab_sems.at[slot]
        )
        copy.start()
        got_vocab.append(copy)

    for b in range(REQUESTS):
        kbuf[b, KEYS + 16 : PADDED, :] = jnp.zeros((PADDED - KEYS - 16, WIDTH), BF16)
    got_parents.wait()
    row = lax.broadcasted_iota(jnp.int32, (TOKENS, TOKENS), 0)
    column = lax.broadcasted_iota(jnp.int32, (TOKENS, TOKENS), 1)
    parent = parents[...]
    first = jnp.where(lax.broadcasted_iota(jnp.int32, (1, TOKENS), 1) >= DRAFT, DRAFT, 0)
    parent = jnp.where(parent < 0, -1, parent + first)
    reach = jnp.where((parent == row) | (row == column), 1.0, 0.0).astype(BF16)
    for _ in range(6):
        reach = jnp.where(dot(reach, reach) > 0.5, 1.0, 0.0).astype(BF16)
    chosen = jnp.where(
        (column < 8)
        & (row == lax.div(column, 4) * DRAFT + seat * 4 + lax.rem(column, 4)),
        1.0,
        0.0,
    )
    reached = dot(reach.astype(F32).T.astype(BF16), chosen.astype(BF16))
    tree_bias = jnp.where(reached > 0.5, 0.0, NEGATIVE)

    got_nope.wait()
    nope32[...] = nope[...].astype(F32)
    got_rope.wait()
    rope32[...] = rope[...].astype(F32)
    got_key.wait()
    for h in range(HEADS):
        picked = nope32[pl.ds(h, TOKENS, stride=HEADS), :].astype(BF16)
        absorbed = dot(picked, key_weight[h]).astype(BF16)
        turned = rope32[pl.ds(h, TOKENS, stride=HEADS), :].astype(BF16)
        for b in range(REQUESTS):
            rows = pl.ds(h * DRAFT, DRAFT)
            qbuf[b, rows, 0:LATENT] = absorbed[b * DRAFT : (b + 1) * DRAFT]
            qbuf[b, rows, LATENT:WIDTH] = turned[b * DRAFT : (b + 1) * DRAFT]

    scale = math.log2(math.e) / math.sqrt(192.0)
    lane = lax.broadcasted_iota(jnp.int32, (DRAFT, 128), 1)
    position = seat * KEYS + lax.broadcasted_iota(jnp.int32, (1, KEYS), 1)
    o_copies, ml_copies, own_copies = [], [], []
    for b in range(REQUESTS):
        got_draft[b].wait()
        got_cache[b].wait()
        if b == 0:
            got_value.wait()
        live_bias = jnp.where(position < lengths[b], 0.0, NEGATIVE)
        tree = tree_bias[b * DRAFT : (b + 1) * DRAFT]
        tops = jnp.zeros((DRAFT, 128), F32)
        totals = jnp.zeros((DRAFT, 128), F32)
        for start in range(0, HEADS * DRAFT, BLOCK):
            rows = pl.ds(start, BLOCK)
            scores = nt_dot(qbuf[b, rows, :], kbuf[b])
            cached = scores[:, :KEYS] + live_bias
            drafted = scores[:, KEYS:] + jnp.concatenate([tree] * (BLOCK // DRAFT), axis=0)
            top = jnp.maximum(
                jnp.max(cached, -1, keepdims=True), jnp.max(drafted, -1, keepdims=True)
            )
            cached = jnp.exp2((cached - top) * scale)
            drafted = jnp.exp2((drafted - top) * scale)
            total = jnp.sum(cached, -1, keepdims=True) + jnp.sum(drafted, -1, keepdims=True)
            pbuf[:, :KEYS] = cached.astype(BF16)
            pbuf[:, KEYS:] = drafted.astype(BF16)
            mixed = dot(pbuf[...], kbuf[b, :, 0:LATENT]).astype(BF16)
            for part in range(BLOCK // DRAFT):
                h = start // DRAFT + part
                sub = slice(part * DRAFT, (part + 1) * DRAFT)
                o_send[b, h] = dot(mixed[sub], value_weight[h]).astype(BF16)
                tops = jnp.where(lane == h, top[sub] * scale, tops)
                totals = jnp.where(lane == h, total[sub], totals)
        turned = jnp.concatenate([tops, totals], axis=0).T
        for h in range(HEADS):
            ml_send[b, h] = turned[h : h + 1]
        if b == 0:
            pl.semaphore_wait(barrier, 30)
        for j, step in enumerate(SEQ_STEPS):
            peer = seq_peers[j]
            there, their_core = lax.div(peer, 2), lax.rem(peer, 2)
            half = pl.ds(pl.multiple_of(their_core * 32, 32), 32)
            copy = pltpu.make_async_remote_copy(
                o_send.at[b, there, half, :],
                o_recv.at[b, j],
                o_sems.at[0, b, j],
                o_sems.at[1, b, j],
                device_id={"seq": peer},
                device_id_type=MESH,
            )
            copy.start()
            o_copies.append(copy)
            copy = pltpu.make_async_remote_copy(
                ml_send.at[b, there],
                ml_recv.at[b, j],
                ml_sems.at[0, b, j],
                ml_sems.at[1, b, j],
                device_id={"seq": peer},
                device_id_type=MESH,
            )
            copy.start()
            ml_copies.append(copy)
        half = pl.ds(pl.multiple_of(core * 32, 32), 32)
        for k, (src, dst) in enumerate(
            ((o_send.at[b, chip, half, :], o_recv.at[b, 15]), (ml_send.at[b, chip], ml_recv.at[b, 15]))
        ):
            copy = pltpu.make_async_copy(src, dst, local_sems.at[b, k])
            copy.start()
            own_copies.append(copy)

    g_copies = []
    for b in range(REQUESTS):
        for copy in ml_copies[b * 15 : (b + 1) * 15]:
            copy.wait_recv()
        for copy in own_copies[b * 2 : (b + 1) * 2]:
            copy.wait()
        gathered = jnp.concatenate(
            [ml_recv[b, j] for j in range(16)] + [jnp.full((112, 128), NEGATIVE, F32)], axis=0
        ).T
        tops, totals = gathered[:DRAFT], gathered[DRAFT:]
        shares = jnp.exp2(tops - jnp.max(tops, -1, keepdims=True))
        shares = shares / jnp.sum(shares * totals, -1, keepdims=True)
        shares = jnp.where(core == 0, shares[:32], shares[32:])
        for copy in o_copies[b * 15 : (b + 1) * 15]:
            copy.wait_recv()
        summed = jnp.zeros((32, 128), F32)
        for j in range(16):
            summed = summed + shares[:, j : j + 1] * o_recv[b, j].astype(F32)
        g_send[b] = summed.astype(BF16)
        place = g_full.at[
            pl.ds(pl.multiple_of(b * DRAFT + core * 32, 32), 32),
            pl.ds(pl.multiple_of(chip * 128, 128), 128),
        ]
        for j, peer in enumerate(seq_peers):
            copy = pltpu.make_async_remote_copy(
                g_send.at[b],
                place,
                g_sems.at[0, b, j],
                g_sems.at[1, b, j],
                device_id={"seq": peer},
                device_id_type=MESH,
            )
            copy.start()
            g_copies.append(copy)
        copy = pltpu.make_async_copy(g_send.at[b], place, local_sems.at[b, 2])
        copy.start()
        own_copies.append(copy)

    got_out.wait()
    for copy in own_copies[4:]:
        copy.wait()
    for copy in g_copies:
        copy.wait_recv()
    attention = dot(g_full[...], out_weight[...]).astype(BF16)
    for i in range(16):
        a_send[i] = attention[i * 8 : (i + 1) * 8]
    a_copies = []
    for j, peer in enumerate(head_peers):
        copy = pltpu.make_async_remote_copy(
            a_send.at[peer],
            a_recv.at[j],
            a_sems.at[0, j],
            a_sems.at[1, j],
            device_id={"head": peer},
            device_id_type=MESH,
        )
        copy.start()
        a_copies.append(copy)
    summed = a_send[mine].astype(F32)
    for j, copy in enumerate(a_copies):
        copy.wait_recv()
        summed = summed + a_recv[j].astype(F32)
    b_send[...] = summed.astype(BF16)
    b_copies = []
    for j, peer in enumerate(head_peers):
        copy = pltpu.make_async_remote_copy(
            b_send,
            b_full.at[mine],
            b_sems.at[0, j],
            b_sems.at[1, j],
            device_id={"head": peer},
            device_id_type=MESH,
        )
        copy.start()
        b_copies.append(copy)
    b_full[mine] = b_send[...]
    got_residual.wait()
    got_gain.wait()
    for copy in b_copies:
        copy.wait_recv()
    attention = jnp.concatenate([b_full[i].astype(F32) for i in range(16)], axis=0)
    hidden = residual[...].astype(F32) + attention

    squares = jnp.sum(hidden * hidden, -1, keepdims=True)
    s_send[...] = jnp.broadcast_to(squares, (TOKENS, 128)).T[0:1]
    s_copies = []
    for j, peer in enumerate(seq_peers):
        copy = pltpu.make_async_remote_copy(
            s_send,
            s_recv.at[j],
            s_sems.at[0, j],
            s_sems.at[1, j],
            device_id={"seq": peer},
            device_id_type=MESH,
        )
        copy.start()
        s_copies.append(copy)
    scaled = (hidden * gain[...].astype(F32)).astype(BF16)

    p_copies = []
    for j in range(8):
        got_vocab[j].wait()
        p_send[j] = dot(scaled, vocab[j]).astype(BF16)
        copy = pltpu.make_async_remote_copy(
            p_send.at[j],
            p_recv.at[j],
            p_sems.at[0, j],
            p_sems.at[1, j],
            device_id={"seq": seq_peers[14]},
            device_id_type=MESH,
        )
        copy.start()
        p_copies.append(copy)
    l_copies = []
    for j in range(8):
        got_vocab[8 + j].wait()
        part = dot(scaled, vocab[8 + j])
        p_copies[j].wait_recv()
        part = part + p_recv[j].astype(F32)
        if j < 7:
            l_send[j] = part.astype(BF16)
            copy = pltpu.make_async_remote_copy(
                l_send.at[j],
                l_recv.at[j],
                l_sems.at[0, j],
                l_sems.at[1, j],
                device_id={"seq": seq_peers[2 * j]},
                device_id_type=MESH,
            )
            copy.start()
            l_copies.append(copy)
    total = s_send[...]
    for j, copy in enumerate(s_copies):
        copy.wait_recv()
        total = total + s_recv[j]
    spread = jnp.broadcast_to(lax.rsqrt(total / model_width + EPSILON), (128, TOKENS)).T
    for j, copy in enumerate(l_copies):
        copy.wait_recv()
        part = part + l_recv[j].astype(F32)
    logits[...] = (part * spread[:, 0:1]).astype(BF16)
    for copy in o_copies + ml_copies + g_copies + a_copies + b_copies + s_copies + p_copies + l_copies:
        copy.wait_send()


def per_device(
    latent_cache,
    draft_latent,
    query_nope,
    query_rope,
    parents,
    lengths,
    key_weight,
    value_weight,
    out_weight,
    residual,
    norm_gain,
    vocab_weight,
):
    local_width = residual.shape[2]
    model_width = local_width * lax.axis_size("seq")
    draft = jnp.pad(draft_latent.reshape(8, WIDTH), ((0, 8), (0, 0)))
    hbm = pl.BlockSpec(memory_space=pl.ANY)
    dma = pltpu.SemaphoreType.DMA
    logits = pl.pallas_call(
        functools.partial(kernel, model_width),
        out_shape=jax.ShapeDtypeStruct((TOKENS, 256), BF16),
        in_specs=[pl.BlockSpec(memory_space=pltpu.SMEM)] + [hbm] * 11,
        out_specs=pl.BlockSpec(memory_space=pltpu.VMEM),
        scratch_shapes=[
            pltpu.VMEM((1, TOKENS), jnp.int32),
            pltpu.VMEM((REQUESTS, PADDED, WIDTH), BF16),
            pltpu.VMEM((TOKENS * HEADS, 128), BF16),
            pltpu.VMEM((TOKENS * HEADS, ROPE), BF16),
            pltpu.VMEM((HEADS, 128, LATENT), BF16),
            pltpu.VMEM((HEADS, LATENT, 128), BF16),
            pltpu.VMEM((1024, local_width), BF16),
            pltpu.VMEM((TOKENS, local_width), BF16),
            pltpu.VMEM((1, local_width), BF16),
            pltpu.VMEM((16, local_width, 256), BF16),
            pltpu.VMEM((TOKENS * HEADS, 128), F32),
            pltpu.VMEM((TOKENS * HEADS, ROPE), F32),
            pltpu.VMEM((REQUESTS, HEADS * DRAFT, WIDTH), BF16),
            pltpu.VMEM((BLOCK, PADDED), BF16),
            pltpu.VMEM((REQUESTS, HEADS, DRAFT, 128), BF16),
            pltpu.VMEM((REQUESTS, 16, 32, 128), BF16),
            pltpu.VMEM((REQUESTS, HEADS, 1, 128), F32),
            pltpu.VMEM((REQUESTS, 16, 1, 128), F32),
            pltpu.VMEM((REQUESTS, 32, 128), BF16),
            pltpu.VMEM((TOKENS, 1024), BF16),
            pltpu.VMEM((16, 8, local_width), BF16),
            pltpu.VMEM((15, 8, local_width), BF16),
            pltpu.VMEM((8, local_width), BF16),
            pltpu.VMEM((16, 8, local_width), BF16),
            pltpu.VMEM((1, TOKENS), F32),
            pltpu.VMEM((15, 1, TOKENS), F32),
            pltpu.VMEM((8, TOKENS, 256), BF16),
            pltpu.VMEM((8, TOKENS, 256), BF16),
            pltpu.VMEM((7, TOKENS, 256), BF16),
            pltpu.VMEM((7, TOKENS, 256), BF16),
            dma((12,)),
            dma((16,)),
            dma((REQUESTS, 3)),
            dma((2, REQUESTS, 15)),
            dma((2, REQUESTS, 15)),
            dma((2, REQUESTS, 15)),
            dma((2, 15)),
            dma((2, 15)),
            dma((2, 15)),
            dma((2, 8)),
            dma((2, 7)),
        ],
        compiler_params=pltpu.CompilerParams(
            collective_id=0, has_side_effects=True, vmem_limit_bytes=60 * 1024 * 1024
        ),
    )(
        lengths,
        parents.reshape(1, TOKENS),
        latent_cache,
        draft,
        query_nope.reshape(TOKENS * HEADS, 128),
        query_rope.reshape(TOKENS * HEADS, ROPE),
        key_weight,
        value_weight,
        out_weight,
        residual.reshape(TOKENS, local_width),
        norm_gain.reshape(1, local_width),
        vocab_weight,
    )
    return logits.reshape(REQUESTS, DRAFT, 256)


def solution(mesh):
    in_specs = (
        P(None, "seq", None),
        P(None, "seq", None),
        P(None, None, "head", None),
        P(None, None, "head", None),
        P(),
        P(),
        P("head", None, None),
        P("head", None, None),
        P("head", "seq"),
        P(None, None, "seq"),
        P("seq"),
        P("seq", "head"),
    )
    out_specs = P(None, None, ("head", "seq"))
    return jax.shard_map(
        per_device, mesh=mesh, in_specs=in_specs, out_specs=out_specs, check_vma=False
    )
```

time: 144 us -> 73 us (0.51)
  blocking collectives: 96.8 us -> 0 us
  Pallas kernels: 0 us -> 57.2 us
  matrix products: 17.7 us -> 0 us
  local copies, waits for them, and re-layouts: 6.36 us -> 15.4 us
  other arithmetic: 8.42 us -> 0 us
  starting transfers between devices: 6.92 us -> 0 us
  waiting for transfers between devices: 6.9 us -> 0 us
    all_to_all x6 -> x0, blocking collectives: 96.8 us -> none  [the longest x3 58.7 us: sent_and_summed(): lax.all_to_all(split_up(array, dim, devices), axis, 0, 0, tiled=True)]
    pallas_call x0 -> x1, Pallas kernels: none -> 57.2 us  [per_device(): pl.pallas_call(functools.partial(kernel, model_width), out_shape=jax.Shap...]
    dot_general x13 -> x0, matrix products: 17.3 us -> none  [the longest x1 6.03 us: per_device(): jnp.einsum('brc,bkc->brk', block, latent_cache, preferred_element_type=jn...]
    all_to_all x1 -> x0, starting transfers between devices: 6.92 us -> none  [sent_to_all(): return lax.all_to_all(copies, axis, split_axis=0, concat_axis=0, tiled=True)]
    all_to_all x1 -> x0, waiting for transfers between devices: 6.9 us -> none  [sent_to_all(): return lax.all_to_all(copies, axis, split_axis=0, concat_axis=0, tiled=True)]
    unnamed x22 -> x3, local copies, waits for them, and re-layouts: 4.62 us -> 11.4 us
    reduce_sum x7 -> x0, other arithmetic: 6.33 us -> none  [the longest x2 5.18 us: per_device(): total = jnp.sum(cache_weights, -1) + jnp.sum(draft_weights, -1)]
    reshape x3, local copies, waits for them, and re-layouts: 0.19 us -> 3.34 us  [the longest x1 1.35 us: per_device(): parents.reshape(1, TOKENS)]
  transfers between devices with their start and end apart: 1 -> 0, of which waited for: 1 -> 0; matrix products, arithmetic and copies ran while one was open for 0% -> 0% of each run, Pallas kernels for 0% -> 0%
where the time goes in v1:
time: 73 us; the launch traced here: 72.6 us
  Pallas kernels  57.2 us (78%)
  local copies, waits for them, and re-layouts  15.4 us (21%)
    pallas_call x1, Pallas kernels, per_device(): pl.pallas_call(functools.partial(kernel, model_width), out_shape=jax.Shap...  57.2 us
    unnamed x3, local copies, waits for them, and re-layouts  11.4 us

profile of v1, /device:TPU:1, one launch (start us, length us, event | category | flops | bytes accessed | tf_op | source)
XLA Modules:
  0.0 72.6 jit_solution(17351876739446378045)
XLA Ops:
  0.0 1.3 %reshape.21.parents_hbm = s32[1,128]{1,0:T(1,128)} reshape(s32[2,64]{1,0:T(2,128)} %param.16) | data formatting | bytes 1024 | tf_op jit(solution)/shard_map/reshape | solution.py:461
  1.3 1.3 %reshape.26.gain_hbm = bf16[1,448]{1,0:T(2,128)(2,1)} reshape(bf16[448]{0:T(512)(128)(2,1)} %param.22) | data formatting | bytes 1792 | tf_op jit(solution)/shard_map/reshape | solution.py:470
  2.6 0.7 reshape.22
  3.3 0.6 pad.4.draft_hbm
  4.0 2.3 %copy.14.out_hbm = bf16[1024,448]{1,0:T(8,128)(2,1)} copy(bf16[1024,448]{0,1:T(8,128)(2,1)} %param.20) | data formatting | bytes 1835008 | tf_op args[8]
  6.2 7.7 %copy.13.cache_hbm = bf16[2,2048,576]{2,1,0:T(8,128)(2,1)} copy(bf16[2,2048,576]{1,2,0:T(8,128)(2,1)} %param.12) | data formatting | bytes 9437184 | tf_op args[0]
  13.9 57.2 %shard_map.118 = bf16[128,256]{1,0:T(8,128)(2,1)} custom-call(s32[2]{0:T(128)} %lengths.1, s32[1,128]{1,0:T(1,128)} %reshape.21.parents_hbm, bf16[2,2048,576]{2,1,0:T(8,128)(2,1)} %copy.13.cache_hbm, bf16[16,576]{1,0:T(8,128)(2,1)} %pad.4.draft_hbm, bf16[1024,128]{1,0:T(8,128)(2,1)} %bitcast.5, bf16[1024,64]{1,0:T(8,128)(2,1)} %bitcast.6, ...), custom_call_target="tpu_custom_call" | custom-call | tf_op jit(solution)/shard_map/pallas_call | solution.py:408
  71.1 1.5 %copy.16 = bf16[2,64,256]{2,1,0:T(8,128)(2,1)} copy(bf16[2,64,256]{2,1,0:T(8,128)(2,1)} %bitcast.4) | data formatting | bytes 131072

commit v2 on v1

--- a/solution.py
+++ b/solution.py
@@ -18,7 +18,7 @@
 SEQ_STEPS = [(dy, dx, dk) for dy, dx in CHIP_STEPS for dk in (0, 1)] + [(0, 0, 1)]
 REQUESTS, DRAFT, HEADS, LATENT, ROPE, WIDTH = 2, 64, 8, 512, 64, 576
 TOKENS = REQUESTS * DRAFT
-KEYS, PADDED = 2048, 2176
+KEYS, EXTRA = 2048, 128
 BLOCK = 256
 
 
@@ -47,6 +47,8 @@
     logits,
     parents,
     kbuf,
+    draft,
+    dbuf,
     nope,
     rope,
     key_weight,
@@ -58,7 +60,6 @@
     nope32,
     rope32,
     qbuf,
-    pbuf,
     o_send,
     o_recv,
     ml_send,
@@ -118,8 +119,8 @@
     got_rope = load(rope_hbm, rope)
     got_key = load(key_hbm, key_weight)
     got_parents = load(parents_hbm, parents)
-    got_draft = [load(draft_hbm, kbuf.at[b, pl.ds(KEYS, 16), :]) for b in range(REQUESTS)]
-    got_cache = [load(cache_hbm.at[b], kbuf.at[b, pl.ds(0, KEYS), :]) for b in range(REQUESTS)]
+    got_draft = load(draft_hbm, draft)
+    got_cache = [load(cache_hbm.at[b], kbuf.at[b]) for b in range(REQUESTS)]
     got_value = load(value_hbm, value_weight)
     got_out = load(out_hbm, out_weight)
     got_residual = load(residual_hbm, residual)
@@ -138,25 +139,28 @@
         copy.start()
         got_vocab.append(copy)
 
+    got_parents.wait()
+    row = lax.broadcasted_iota(jnp.int32, (DRAFT, DRAFT), 0)
+    column = lax.broadcasted_iota(jnp.int32, (DRAFT, DRAFT), 1)
+    reaches = [
+        jnp.where((parents[b : b + 1, :] == row) | (row == column), 1.0, 0.0).astype(BF16)
+        for b in range(REQUESTS)
+    ]
+    for _ in range(6):
+        reaches = [jnp.where(dot(r, r) > 0.5, 1.0, 0.0).astype(BF16) for r in reaches]
+    row = lax.broadcasted_iota(jnp.int32, (DRAFT, EXTRA), 0)
+    column = lax.broadcasted_iota(jnp.int32, (DRAFT, EXTRA), 1)
+    tree_bias = []
     for b in range(REQUESTS):
-        kbuf[b, KEYS + 16 : PADDED, :] = jnp.zeros((PADDED - KEYS - 16, WIDTH), BF16)
-    got_parents.wait()
-    row = lax.broadcasted_iota(jnp.int32, (TOKENS, TOKENS), 0)
-    column = lax.broadcasted_iota(jnp.int32, (TOKENS, TOKENS), 1)
-    parent = parents[...]
-    first = jnp.where(lax.broadcasted_iota(jnp.int32, (1, TOKENS), 1) >= DRAFT, DRAFT, 0)
-    parent = jnp.where(parent < 0, -1, parent + first)
-    reach = jnp.where((parent == row) | (row == column), 1.0, 0.0).astype(BF16)
-    for _ in range(6):
-        reach = jnp.where(dot(reach, reach) > 0.5, 1.0, 0.0).astype(BF16)
-    chosen = jnp.where(
-        (column < 8)
-        & (row == lax.div(column, 4) * DRAFT + seat * 4 + lax.rem(column, 4)),
-        1.0,
-        0.0,
-    )
-    reached = dot(reach.astype(F32).T.astype(BF16), chosen.astype(BF16))
-    tree_bias = jnp.where(reached > 0.5, 0.0, NEGATIVE)
+        chosen = (column >= 4 * b) & (column < 4 * b + 4) & (row == seat * 4 + column - 4 * b)
+        chosen = jnp.where(chosen, 1.0, 0.0).astype(BF16)
+        reached = lax.dot_general(
+            reaches[b], chosen, (((0,), (0,)), ((), ())), preferred_element_type=F32
+        )
+        tree_bias.append(jnp.where(reached > 0.5, 0.0, NEGATIVE))
+    got_draft.wait()
+    dbuf[...] = jnp.zeros((EXTRA, WIDTH), BF16)
+    dbuf[0:8, :] = jnp.concatenate([draft[b].astype(F32) for b in range(REQUESTS)], axis=0).astype(BF16)
 
     got_nope.wait()
     nope32[...] = nope[...].astype(F32)
@@ -177,28 +181,25 @@
     position = seat * KEYS + lax.broadcasted_iota(jnp.int32, (1, KEYS), 1)
     o_copies, ml_copies, own_copies = [], [], []
     for b in range(REQUESTS):
-        got_draft[b].wait()
         got_cache[b].wait()
         if b == 0:
             got_value.wait()
         live_bias = jnp.where(position < lengths[b], 0.0, NEGATIVE)
-        tree = tree_bias[b * DRAFT : (b + 1) * DRAFT]
+        tree = jnp.concatenate([tree_bias[b]] * (BLOCK // DRAFT), axis=0)
         tops = jnp.zeros((DRAFT, 128), F32)
         totals = jnp.zeros((DRAFT, 128), F32)
         for start in range(0, HEADS * DRAFT, BLOCK):
             rows = pl.ds(start, BLOCK)
-            scores = nt_dot(qbuf[b, rows, :], kbuf[b])
-            cached = scores[:, :KEYS] + live_bias
-            drafted = scores[:, KEYS:] + jnp.concatenate([tree] * (BLOCK // DRAFT), axis=0)
+            cached = dot(qbuf[b, rows, :], kbuf[b]) + live_bias
+            drafted = nt_dot(qbuf[b, rows, :], dbuf[...]) + tree
             top = jnp.maximum(
                 jnp.max(cached, -1, keepdims=True), jnp.max(drafted, -1, keepdims=True)
             )
             cached = jnp.exp2((cached - top) * scale)
             drafted = jnp.exp2((drafted - top) * scale)
             total = jnp.sum(cached, -1, keepdims=True) + jnp.sum(drafted, -1, keepdims=True)
-            pbuf[:, :KEYS] = cached.astype(BF16)
-            pbuf[:, KEYS:] = drafted.astype(BF16)
-            mixed = dot(pbuf[...], kbuf[b, :, 0:LATENT]).astype(BF16)
+            mixed = nt_dot(cached.astype(BF16), kbuf[b, 0:LATENT, :])
+            mixed = (mixed + dot(drafted.astype(BF16), dbuf[:, 0:LATENT])).astype(BF16)
             for part in range(BLOCK // DRAFT):
                 h = start // DRAFT + part
                 sub = slice(part * DRAFT, (part + 1) * DRAFT)
@@ -285,7 +286,7 @@
         copy.wait()
     for copy in g_copies:
         copy.wait_recv()
-    attention = dot(g_full[...], out_weight[...]).astype(BF16)
+    attention = nt_dot(g_full[...], out_weight[...]).astype(BF16)
     for i in range(16):
         a_send[i] = attention[i * 8 : (i + 1) * 8]
     a_copies = []
@@ -339,7 +340,7 @@
         )
         copy.start()
         s_copies.append(copy)
-    scaled = (hidden * gain[...].astype(F32)).astype(BF16)
+    scaled = (hidden * gain[...].astype(F32)[None, :]).astype(BF16)
 
     p_copies = []
     for j in range(8):
@@ -402,7 +403,6 @@
 ):
     local_width = residual.shape[2]
     model_width = local_width * lax.axis_size("seq")
-    draft = jnp.pad(draft_latent.reshape(8, WIDTH), ((0, 8), (0, 0)))
     hbm = pl.BlockSpec(memory_space=pl.ANY)
     dma = pltpu.SemaphoreType.DMA
     logits = pl.pallas_call(
@@ -411,20 +411,21 @@
         in_specs=[pl.BlockSpec(memory_space=pltpu.SMEM)] + [hbm] * 11,
         out_specs=pl.BlockSpec(memory_space=pltpu.VMEM),
         scratch_shapes=[
-            pltpu.VMEM((1, TOKENS), jnp.int32),
-            pltpu.VMEM((REQUESTS, PADDED, WIDTH), BF16),
+            pltpu.VMEM((REQUESTS, DRAFT), jnp.int32),
+            pltpu.VMEM((REQUESTS, WIDTH, KEYS), BF16),
+            pltpu.VMEM((REQUESTS, 4, WIDTH), BF16),
+            pltpu.VMEM((EXTRA, WIDTH), BF16),
             pltpu.VMEM((TOKENS * HEADS, 128), BF16),
             pltpu.VMEM((TOKENS * HEADS, ROPE), BF16),
             pltpu.VMEM((HEADS, 128, LATENT), BF16),
             pltpu.VMEM((HEADS, LATENT, 128), BF16),
-            pltpu.VMEM((1024, local_width), BF16),
+            pltpu.VMEM((local_width, 1024), BF16),
             pltpu.VMEM((TOKENS, local_width), BF16),
-            pltpu.VMEM((1, local_width), BF16),
+            pltpu.VMEM((local_width,), BF16),
             pltpu.VMEM((16, local_width, 256), BF16),
             pltpu.VMEM((TOKENS * HEADS, 128), F32),
             pltpu.VMEM((TOKENS * HEADS, ROPE), F32),
             pltpu.VMEM((REQUESTS, HEADS * DRAFT, WIDTH), BF16),
-            pltpu.VMEM((BLOCK, PADDED), BF16),
             pltpu.VMEM((REQUESTS, HEADS, DRAFT, 128), BF16),
             pltpu.VMEM((REQUESTS, 16, 32, 128), BF16),
             pltpu.VMEM((REQUESTS, HEADS, 1, 128), F32),
@@ -458,16 +459,16 @@
         ),
     )(
         lengths,
-        parents.reshape(1, TOKENS),
-        latent_cache,
-        draft,
+        parents,
+        jnp.swapaxes(latent_cache, 1, 2),
+        draft_latent,
         query_nope.reshape(TOKENS * HEADS, 128),
         query_rope.reshape(TOKENS * HEADS, ROPE),
         key_weight,
         value_weight,
-        out_weight,
+        out_weight.T,
         residual.reshape(TOKENS, local_width),
-        norm_gain.reshape(1, local_width),
+        norm_gain,
         vocab_weight,
     )
     return logits.reshape(REQUESTS, DRAFT, 256)

time: 73 us -> 60.8 us (0.83)
  local copies, waits for them, and re-layouts: 15.4 us -> 1.47 us
  Pallas kernels: 57.2 us -> 59.2 us
    unnamed x3 -> x1, local copies, waits for them, and re-layouts: 11.4 us -> 1.47 us
    reshape x3 -> x0, local copies, waits for them, and re-layouts: 3.34 us -> none  [the longest x1 1.35 us: per_device(): parents.reshape(1, TOKENS)]
    pallas_call x1, Pallas kernels: 57.2 us -> 59.2 us  [per_device(): pl.pallas_call(functools.partial(kernel, model_width), out_shape=jax.Shap...]
where the time goes in v2:
time: 60.8 us; the launch traced here: 60.7 us
  Pallas kernels  59.2 us (97%)
  local copies, waits for them, and re-layouts  1.47 us (2%)
    pallas_call x1, Pallas kernels, per_device(): pl.pallas_call(functools.partial(kernel, model_width), out_shape=jax.Shap...  59.2 us
    unnamed x1, local copies, waits for them, and re-layouts  1.47 us

profile of v2, /device:TPU:1, one launch (start us, length us, event | category | flops | bytes accessed | tf_op | source)
XLA Modules:
  0.0 60.7 jit_solution(5107622144220716693)
XLA Ops:
  0.0 59.2 %shard_map.118 = bf16[128,256]{1,0:T(8,128)(2,1)} custom-call(s32[2]{0:T(128)} %lengths.1, s32[2,64]{1,0:T(2,128)} %parents_hbm.1, bf16[2,576,2048]{2,1,0:T(8,128)(2,1)} %bitcast.6, bf16[2,4,576]{2,1,0:T(4,128)(2,1)} %draft_hbm.1, bf16[1024,128]{1,0:T(8,128)(2,1)} %bitcast.9, bf16[1024,64]{1,0:T(8,128)(2,1)} %bitcast.10, bf16[8,128,512]{2,1,0:T(8,128)(2,1)} %key_hbm.1, ...), custom_call_target="tpu_custom_call" | custom-call | tf_op jit(solution)/shard_map/pallas_call | solution.py:408
  59.2 1.5 %copy.14 = bf16[2,64,256]{2,1,0:T(8,128)(2,1)} copy(bf16[2,64,256]{2,1,0:T(8,128)(2,1)} %bitcast.8) | data formatting | bytes 131072

commit v3 on v2

--- a/solution.py
+++ b/solution.py
@@ -19,7 +19,8 @@
 REQUESTS, DRAFT, HEADS, LATENT, ROPE, WIDTH = 2, 64, 8, 512, 64, 576
 TOKENS = REQUESTS * DRAFT
 KEYS, EXTRA = 2048, 128
-BLOCK = 256
+HALF = DRAFT // 2
+BLOCK = 512
 
 
 def nt_dot(a, b):
@@ -56,6 +57,7 @@
     out_weight,
     residual,
     gain,
+    gain_rows,
     vocab,
     nope32,
     rope32,
@@ -72,8 +74,6 @@
     b_full,
     s_send,
     s_recv,
-    p_send,
-    p_recv,
     l_send,
     l_recv,
     load_sems,
@@ -85,7 +85,7 @@
     a_sems,
     b_sems,
     s_sems,
-    p_sems,
+    swap_sems,
     l_sems,
 ):
     seat = lax.axis_index("seq")
@@ -99,6 +99,7 @@
         return lax.rem(y + dy, 4) * 4 + lax.rem(xh + dx, 2) * 2 + lax.rem(core + dk, 2)
 
     seq_peers = [seat_at(*step) for step in SEQ_STEPS]
+    chip_peers = seq_peers[0:14:2]
     head_peers = [lax.rem(mine + j, 16) for j in range(1, 16)]
 
     barrier = pltpu.get_barrier_semaphore()
@@ -122,19 +123,22 @@
     got_draft = load(draft_hbm, draft)
     got_cache = [load(cache_hbm.at[b], kbuf.at[b]) for b in range(REQUESTS)]
     got_value = load(value_hbm, value_weight)
-    got_out = load(out_hbm, out_weight)
-    got_residual = load(residual_hbm, residual)
+    got_out = load(out_hbm, out_weight.at[core])
+    got_residual = [
+        load(
+            residual_hbm.at[pl.ds(pl.multiple_of(b * DRAFT + core * HALF, HALF), HALF), :],
+            residual.at[core, pl.ds(b * HALF, HALF), :],
+        )
+        for b in range(REQUESTS)
+    ]
     got_gain = load(gain_hbm, gain)
 
-    vocab_order = []
-    for half in (1, 0):
-        for dy, dx in CHIP_STEPS + [(0, 0)]:
-            vocab_order.append(seat_at(dy, dx, half))
     got_vocab = []
-    for slot, owner in enumerate(vocab_order):
-        columns = pl.ds(pl.multiple_of(owner * 256, 256), 256)
+    for slot, (dy, dx) in enumerate(CHIP_STEPS + [(0, 0)]):
+        owner = lax.div(seat_at(dy, dx, 0), 2)
+        columns = pl.ds(pl.multiple_of(owner * 512, 512), 512)
         copy = pltpu.make_async_copy(
-            vocab_hbm.at[:, columns], vocab.at[slot], vocab_sems.at[slot]
+            vocab_hbm.at[:, columns], vocab.at[core, slot], vocab_sems.at[slot]
         )
         copy.start()
         got_vocab.append(copy)
@@ -179,7 +183,8 @@
     scale = math.log2(math.e) / math.sqrt(192.0)
     lane = lax.broadcasted_iota(jnp.int32, (DRAFT, 128), 1)
     position = seat * KEYS + lax.broadcasted_iota(jnp.int32, (1, KEYS), 1)
-    o_copies, ml_copies, own_copies = [], [], []
+    o_copies, ml_copies, own_copies, swap_copies = [], [], [], []
+    partner = seq_peers[14]
     for b in range(REQUESTS):
         got_cache[b].wait()
         if b == 0:
@@ -235,6 +240,37 @@
             )
             copy.start()
             ml_copies.append(copy)
+        swaps = []
+        if b == 0:
+            got_out.wait()
+            got_gain.wait()
+            gain_rows[core] = gain[...].astype(F32)[None, :]
+            swaps.append((out_weight.at[core], out_weight.at[core], 0))
+            swaps.append((gain_rows.at[core], gain_rows.at[core], 1))
+            for request in range(REQUESTS):
+                other_rows = pl.multiple_of(request * DRAFT + (1 - core) * HALF, HALF)
+                swaps.append(
+                    (
+                        residual_hbm.at[pl.ds(other_rows, HALF), :],
+                        residual.at[core, pl.ds(request * HALF, HALF), :],
+                        2 + request,
+                    )
+                )
+        else:
+            for slot in range(8):
+                got_vocab[slot].wait()
+                swaps.append((vocab.at[core, slot], vocab.at[core, slot], 4 + slot))
+        for src, dst, k in swaps:
+            copy = pltpu.make_async_remote_copy(
+                src,
+                dst,
+                swap_sems.at[0, k],
+                swap_sems.at[1, k],
+                device_id={"seq": partner},
+                device_id_type=MESH,
+            )
+            copy.start()
+            swap_copies.append(copy)
         half = pl.ds(pl.multiple_of(core * 32, 32), 32)
         for k, (src, dst) in enumerate(
             ((o_send.at[b, chip, half, :], o_recv.at[b, 15]), (ml_send.at[b, chip], ml_recv.at[b, 15]))
@@ -263,10 +299,10 @@
             summed = summed + shares[:, j : j + 1] * o_recv[b, j].astype(F32)
         g_send[b] = summed.astype(BF16)
         place = g_full.at[
-            pl.ds(pl.multiple_of(b * DRAFT + core * 32, 32), 32),
+            pl.ds(b * HALF, HALF),
             pl.ds(pl.multiple_of(chip * 128, 128), 128),
         ]
-        for j, peer in enumerate(seq_peers):
+        for j, peer in enumerate(chip_peers):
             copy = pltpu.make_async_remote_copy(
                 g_send.at[b],
                 place,
@@ -281,14 +317,15 @@
         copy.start()
         own_copies.append(copy)
 
-    got_out.wait()
     for copy in own_copies[4:]:
         copy.wait()
+    swap_copies[0].wait_recv()
     for copy in g_copies:
         copy.wait_recv()
-    attention = nt_dot(g_full[...], out_weight[...]).astype(BF16)
-    for i in range(16):
-        a_send[i] = attention[i * 8 : (i + 1) * 8]
+    for side in range(2):
+        attention = nt_dot(g_full[...], out_weight[side]).astype(BF16)
+        for i in range(8):
+            a_send[2 * i + side] = attention[i * 8 : (i + 1) * 8]
     a_copies = []
     for j, peer in enumerate(head_peers):
         copy = pltpu.make_async_remote_copy(
@@ -319,15 +356,23 @@
         copy.start()
         b_copies.append(copy)
     b_full[mine] = b_send[...]
-    got_residual.wait()
-    got_gain.wait()
+    for copy in got_residual:
+        copy.wait()
+    for copy in swap_copies[1:4]:
+        copy.wait_recv()
     for copy in b_copies:
         copy.wait_recv()
-    attention = jnp.concatenate([b_full[i].astype(F32) for i in range(16)], axis=0)
-    hidden = residual[...].astype(F32) + attention
-
-    squares = jnp.sum(hidden * hidden, -1, keepdims=True)
-    s_send[...] = jnp.broadcast_to(squares, (TOKENS, 128)).T[0:1]
+    squares = jnp.zeros((2 * HALF, 1), F32)
+    scaled = []
+    for side in range(2):
+        attention = jnp.concatenate(
+            [b_full[2 * i + side].astype(F32) for i in range(8)], axis=0
+        )
+        hidden = residual[side].astype(F32) + attention
+        squares = squares + jnp.sum(hidden * hidden, -1, keepdims=True)
+        scaled.append((hidden * gain_rows[side]).astype(BF16))
+
+    s_send[...] = jnp.broadcast_to(jnp.concatenate([squares] * 2, axis=0), (TOKENS, 128)).T[0:1]
     s_copies = []
     for j, peer in enumerate(seq_peers):
         copy = pltpu.make_async_remote_copy(
@@ -340,50 +385,46 @@
         )
         copy.start()
         s_copies.append(copy)
-    scaled = (hidden * gain[...].astype(F32)[None, :]).astype(BF16)
-
-    p_copies = []
-    for j in range(8):
-        got_vocab[j].wait()
-        p_send[j] = dot(scaled, vocab[j]).astype(BF16)
-        copy = pltpu.make_async_remote_copy(
-            p_send.at[j],
-            p_recv.at[j],
-            p_sems.at[0, j],
-            p_sems.at[1, j],
-            device_id={"seq": seq_peers[14]},
-            device_id_type=MESH,
-        )
-        copy.start()
-        p_copies.append(copy)
     l_copies = []
-    for j in range(8):
-        got_vocab[8 + j].wait()
-        part = dot(scaled, vocab[8 + j])
-        p_copies[j].wait_recv()
-        part = part + p_recv[j].astype(F32)
-        if j < 7:
-            l_send[j] = part.astype(BF16)
+    for slot in range(8):
+        swap_copies[4 + slot].wait_recv()
+        part = dot(scaled[0], vocab[0, slot]) + dot(scaled[1], vocab[1, slot])
+        for side in range(2):
+            l_send[slot, side] = part[:, side * 256 : (side + 1) * 256].astype(BF16)
+        for dk in range(2):
+            j = 2 * slot + dk
+            if slot == 7:
+                if dk == 0:
+                    continue
+                j = 14
             copy = pltpu.make_async_remote_copy(
-                l_send.at[j],
+                l_send.at[slot, lax.rem(core + dk, 2)],
                 l_recv.at[j],
                 l_sems.at[0, j],
                 l_sems.at[1, j],
-                device_id={"seq": seq_peers[2 * j]},
+                device_id={"seq": seq_peers[j]},
                 device_id_type=MESH,
             )
             copy.start()
             l_copies.append(copy)
-    total = s_send[...]
-    for j, copy in enumerate(s_copies):
-        copy.wait_recv()
-        total = total + s_recv[j]
-    spread = jnp.broadcast_to(lax.rsqrt(total / model_width + EPSILON), (128, TOKENS)).T
-    for j, copy in enumerate(l_copies):
-        copy.wait_recv()
-        part = part + l_recv[j].astype(F32)
-    logits[...] = (part * spread[:, 0:1]).astype(BF16)
-    for copy in o_copies + ml_copies + g_copies + a_copies + b_copies + s_copies + p_copies + l_copies:
+    sums = [l_send[7, core].astype(F32), jnp.zeros((2 * HALF, 256), F32)]
+    squares = [s_send[...], jnp.zeros((1, TOKENS), F32)]
+    for j, (_, _, dk) in enumerate(SEQ_STEPS):
+        s_copies[j].wait_recv()
+        squares[dk] = squares[dk] + s_recv[j]
+    for j, (_, _, dk) in enumerate(SEQ_STEPS):
+        l_copies[j].wait_recv()
+        sums[dk] = sums[dk] + l_recv[j].astype(F32)
+    for dk in range(2):
+        scales = jnp.broadcast_to(
+            lax.rsqrt(squares[dk] / model_width + EPSILON), (128, TOKENS)
+        ).T
+        done = (sums[dk] * scales[: 2 * HALF, 0:1]).astype(BF16)
+        owner = lax.rem(core + dk, 2)
+        for b in range(REQUESTS):
+            rows = pl.ds(pl.multiple_of(b * DRAFT + owner * HALF, HALF), HALF)
+            logits[rows, :] = done[b * HALF : (b + 1) * HALF]
+    for copy in o_copies + ml_copies + swap_copies + g_copies + a_copies + b_copies + s_copies + l_copies:
         copy.wait_send()
 
 
@@ -419,10 +460,11 @@
             pltpu.VMEM((TOKENS * HEADS, ROPE), BF16),
             pltpu.VMEM((HEADS, 128, LATENT), BF16),
             pltpu.VMEM((HEADS, LATENT, 128), BF16),
-            pltpu.VMEM((local_width, 1024), BF16),
-            pltpu.VMEM((TOKENS, local_width), BF16),
+            pltpu.VMEM((2, local_width, 1024), BF16),
+            pltpu.VMEM((2, 2 * HALF, local_width), BF16),
             pltpu.VMEM((local_width,), BF16),
-            pltpu.VMEM((16, local_width, 256), BF16),
+            pltpu.VMEM((2, 1, local_width), F32),
+            pltpu.VMEM((2, 8, local_width, 512), BF16),
             pltpu.VMEM((TOKENS * HEADS, 128), F32),
             pltpu.VMEM((TOKENS * HEADS, ROPE), F32),
             pltpu.VMEM((REQUESTS, HEADS * DRAFT, WIDTH), BF16),
@@ -431,28 +473,26 @@
             pltpu.VMEM((REQUESTS, HEADS, 1, 128), F32),
             pltpu.VMEM((REQUESTS, 16, 1, 128), F32),
             pltpu.VMEM((REQUESTS, 32, 128), BF16),
-            pltpu.VMEM((TOKENS, 1024), BF16),
+            pltpu.VMEM((2 * HALF, 1024), BF16),
             pltpu.VMEM((16, 8, local_width), BF16),
             pltpu.VMEM((15, 8, local_width), BF16),
             pltpu.VMEM((8, local_width), BF16),
             pltpu.VMEM((16, 8, local_width), BF16),
             pltpu.VMEM((1, TOKENS), F32),
             pltpu.VMEM((15, 1, TOKENS), F32),
-            pltpu.VMEM((8, TOKENS, 256), BF16),
-            pltpu.VMEM((8, TOKENS, 256), BF16),
-            pltpu.VMEM((7, TOKENS, 256), BF16),
-            pltpu.VMEM((7, TOKENS, 256), BF16),
+            pltpu.VMEM((8, 2, 2 * HALF, 256), BF16),
+            pltpu.VMEM((15, 2 * HALF, 256), BF16),
             dma((12,)),
-            dma((16,)),
+            dma((8,)),
             dma((REQUESTS, 3)),
             dma((2, REQUESTS, 15)),
             dma((2, REQUESTS, 15)),
-            dma((2, REQUESTS, 15)),
+            dma((2, REQUESTS, 7)),
             dma((2, 15)),
             dma((2, 15)),
             dma((2, 15)),
-            dma((2, 8)),
-            dma((2, 7)),
+            dma((2, 12)),
+            dma((2, 15)),
         ],
         compiler_params=pltpu.CompilerParams(
             collective_id=0, has_side_effects=True, vmem_limit_bytes=60 * 1024 * 1024

time: 60.8 us -> 56.2 us (0.924)
  Pallas kernels: 59.2 us -> 54.5 us
    pallas_call x1, Pallas kernels: 59.2 us -> 54.5 us  [per_device(): pl.pallas_call(functools.partial(kernel, model_width), out_shape=jax.Shap...]
where the time goes in v3:
time: 56.2 us; the launch traced here: 56 us
  Pallas kernels  54.5 us (97%)
  local copies, waits for them, and re-layouts  1.47 us (3%)
    pallas_call x1, Pallas kernels, per_device(): pl.pallas_call(functools.partial(kernel, model_width), out_shape=jax.Shap...  54.5 us
    unnamed x1, local copies, waits for them, and re-layouts  1.47 us

profile of v3, /device:TPU:1, one launch (start us, length us, event | category | flops | bytes accessed | tf_op | source)
XLA Modules:
  0.0 56.0 jit_solution(17984416544100090998)
XLA Ops:
  0.0 54.5 %shard_map.118 = bf16[128,256]{1,0:T(8,128)(2,1)} custom-call(s32[2]{0:T(128)} %lengths.1, s32[2,64]{1,0:T(2,128)} %parents_hbm.1, bf16[2,576,2048]{2,1,0:T(8,128)(2,1)} %bitcast.6, bf16[2,4,576]{2,1,0:T(4,128)(2,1)} %draft_hbm.1, bf16[1024,128]{1,0:T(8,128)(2,1)} %bitcast.9, bf16[1024,64]{1,0:T(8,128)(2,1)} %bitcast.10, bf16[8,128,512]{2,1,0:T(8,128)(2,1)} %key_hbm.1, ...), custom_call_target="tpu_custom_call" | custom-call | tf_op jit(solution)/shard_map/pallas_call | solution.py:449
  54.6 1.5 %copy.14 = bf16[2,64,256]{2,1,0:T(8,128)(2,1)} copy(bf16[2,64,256]{2,1,0:T(8,128)(2,1)} %bitcast.8) | data formatting | bytes 131072

commit v4 on v3

--- a/solution.py
+++ b/solution.py
@@ -20,7 +20,6 @@
 TOKENS = REQUESTS * DRAFT
 KEYS, EXTRA = 2048, 128
 HALF = DRAFT // 2
-BLOCK = 512
 
 
 def nt_dot(a, b):
@@ -33,7 +32,7 @@
 
 def kernel(
     model_width,
-    lengths,
+    lengths_hbm,
     parents_hbm,
     cache_hbm,
     draft_hbm,
@@ -46,6 +45,7 @@
     gain_hbm,
     vocab_hbm,
     logits,
+    lengths,
     parents,
     kbuf,
     draft,
@@ -116,6 +116,7 @@
         copy.start()
         return copy
 
+    got_lengths = load(lengths_hbm, lengths)
     got_nope = load(nope_hbm, nope)
     got_rope = load(rope_hbm, rope)
     got_key = load(key_hbm, key_weight)
@@ -185,32 +186,33 @@
     position = seat * KEYS + lax.broadcasted_iota(jnp.int32, (1, KEYS), 1)
     o_copies, ml_copies, own_copies, swap_copies = [], [], [], []
     partner = seq_peers[14]
+
+    def score(b):
+        got_cache[b].wait()
+        live_bias = jnp.where(position < lengths[b], 0.0, NEGATIVE)
+        tree = jnp.concatenate([tree_bias[b]] * HEADS, axis=0)
+        return dot(qbuf[b], kbuf[b]) + live_bias, nt_dot(qbuf[b], dbuf[...]) + tree
+
+    got_lengths.wait()
+    got_value.wait()
+    scores = [score(0), score(1)]
     for b in range(REQUESTS):
-        got_cache[b].wait()
-        if b == 0:
-            got_value.wait()
-        live_bias = jnp.where(position < lengths[b], 0.0, NEGATIVE)
-        tree = jnp.concatenate([tree_bias[b]] * (BLOCK // DRAFT), axis=0)
         tops = jnp.zeros((DRAFT, 128), F32)
         totals = jnp.zeros((DRAFT, 128), F32)
-        for start in range(0, HEADS * DRAFT, BLOCK):
-            rows = pl.ds(start, BLOCK)
-            cached = dot(qbuf[b, rows, :], kbuf[b]) + live_bias
-            drafted = nt_dot(qbuf[b, rows, :], dbuf[...]) + tree
-            top = jnp.maximum(
-                jnp.max(cached, -1, keepdims=True), jnp.max(drafted, -1, keepdims=True)
-            )
-            cached = jnp.exp2((cached - top) * scale)
-            drafted = jnp.exp2((drafted - top) * scale)
-            total = jnp.sum(cached, -1, keepdims=True) + jnp.sum(drafted, -1, keepdims=True)
-            mixed = nt_dot(cached.astype(BF16), kbuf[b, 0:LATENT, :])
-            mixed = (mixed + dot(drafted.astype(BF16), dbuf[:, 0:LATENT])).astype(BF16)
-            for part in range(BLOCK // DRAFT):
-                h = start // DRAFT + part
-                sub = slice(part * DRAFT, (part + 1) * DRAFT)
-                o_send[b, h] = dot(mixed[sub], value_weight[h]).astype(BF16)
-                tops = jnp.where(lane == h, top[sub] * scale, tops)
-                totals = jnp.where(lane == h, total[sub], totals)
+        cached, drafted = scores[b]
+        top = jnp.maximum(
+            jnp.max(cached, -1, keepdims=True), jnp.max(drafted, -1, keepdims=True)
+        )
+        cached = jnp.exp2((cached - top) * scale)
+        drafted = jnp.exp2((drafted - top) * scale)
+        total = jnp.sum(cached, -1, keepdims=True) + jnp.sum(drafted, -1, keepdims=True)
+        mixed = nt_dot(cached.astype(BF16), kbuf[b, 0:LATENT, :])
+        mixed = (mixed + dot(drafted.astype(BF16), dbuf[:, 0:LATENT])).astype(BF16)
+        for h in range(HEADS):
+            sub = slice(h * DRAFT, (h + 1) * DRAFT)
+            o_send[b, h] = dot(mixed[sub], value_weight[h]).astype(BF16)
+            tops = jnp.where(lane == h, top[sub] * scale, tops)
+            totals = jnp.where(lane == h, total[sub], totals)
         turned = jnp.concatenate([tops, totals], axis=0).T
         for h in range(HEADS):
             ml_send[b, h] = turned[h : h + 1]
@@ -444,14 +446,29 @@
 ):
     local_width = residual.shape[2]
     model_width = local_width * lax.axis_size("seq")
-    hbm = pl.BlockSpec(memory_space=pl.ANY)
+    operands = [
+        lengths,
+        parents,
+        jnp.swapaxes(latent_cache, 1, 2),
+        draft_latent,
+        query_nope.reshape(TOKENS * HEADS, 128),
+        query_rope.reshape(TOKENS * HEADS, ROPE),
+        key_weight,
+        value_weight,
+        out_weight.T,
+        residual.reshape(TOKENS, local_width),
+        norm_gain,
+        vocab_weight,
+    ]
+    hbm = pl.BlockSpec(memory_space=pltpu.HBM)
     dma = pltpu.SemaphoreType.DMA
     logits = pl.pallas_call(
         functools.partial(kernel, model_width),
         out_shape=jax.ShapeDtypeStruct((TOKENS, 256), BF16),
-        in_specs=[pl.BlockSpec(memory_space=pltpu.SMEM)] + [hbm] * 11,
+        in_specs=[hbm] * 12,
         out_specs=pl.BlockSpec(memory_space=pltpu.VMEM),
         scratch_shapes=[
+            pltpu.SMEM((REQUESTS,), jnp.int32),
             pltpu.VMEM((REQUESTS, DRAFT), jnp.int32),
             pltpu.VMEM((REQUESTS, WIDTH, KEYS), BF16),
             pltpu.VMEM((REQUESTS, 4, WIDTH), BF16),
@@ -482,7 +499,7 @@
             pltpu.VMEM((15, 1, TOKENS), F32),
             pltpu.VMEM((8, 2, 2 * HALF, 256), BF16),
             pltpu.VMEM((15, 2 * HALF, 256), BF16),
-            dma((12,)),
+            dma((16,)),
             dma((8,)),
             dma((REQUESTS, 3)),
             dma((2, REQUESTS, 15)),
@@ -495,21 +512,10 @@
             dma((2, 15)),
         ],
         compiler_params=pltpu.CompilerParams(
-            collective_id=0, has_side_effects=True, vmem_limit_bytes=60 * 1024 * 1024
+            collective_id=0, has_side_effects=True, vmem_limit_bytes=48 * 1024 * 1024
         ),
     )(
-        lengths,
-        parents,
-        jnp.swapaxes(latent_cache, 1, 2),
-        draft_latent,
-        query_nope.reshape(TOKENS * HEADS, 128),
-        query_rope.reshape(TOKENS * HEADS, ROPE),
-        key_weight,
-        value_weight,
-        out_weight.T,
-        residual.reshape(TOKENS, local_width),
-        norm_gain,
-        vocab_weight,
+        *[pltpu.with_memory_space_constraint(a, pltpu.HBM) for a in operands],
     )
     return logits.reshape(REQUESTS, DRAFT, 256)
 

time: 56.2 us -> 51.1 us (0.909)
  Pallas kernels: 54.5 us -> 50.4 us
  local copies, waits for them, and re-layouts: 1.47 us -> 0.63 us
    pallas_call x1, Pallas kernels: 54.5 us -> 50.4 us  [per_device(): pl.pallas_call(functools.partial(kernel, model_width), out_shape=jax.Shap...]
    unnamed x1, local copies, waits for them, and re-layouts: 1.47 us -> 0.63 us
where the time goes in v4:
time: 51.1 us
  Pallas kernels  50.4 us (99%)
  local copies, waits for them, and re-layouts  0.63 us (1%)
    pallas_call x1, Pallas kernels, per_device(): pl.pallas_call(functools.partial(kernel, model_width), out_shape=jax.Shap...  50.4 us

profile of v4, /device:TPU:1, one launch (start us, length us, event | category | flops | bytes accessed | tf_op | source)
XLA Modules:
  0.0 51.1 jit_solution(16652542583336674464)
XLA Ops:
  0.0 50.4 %shard_map.118 = bf16[128,256]{1,0:T(8,128)(2,1)S(1)} custom-call(s32[2]{0:T(128)} %lengths_hbm.1, s32[2,64]{1,0:T(2,128)} %parents_hbm.1, bf16[2,576,2048]{2,1,0:T(8,128)(2,1)} %bitcast.7, bf16[2,4,576]{2,1,0:T(4,128)(2,1)} %draft_hbm.1, bf16[1024,128]{1,0:T(8,128)(2,1)} %bitcast.9, bf16[1024,64]{1,0:T(8,128)(2,1)} %bitcast.10, ...), custom_call_target="tpu_custom_call" | custom-call | tf_op jit(solution)/shard_map/pallas_call | solution.py:465
  50.4 0.6 %copy.14 = bf16[2,64,256]{2,1,0:T(8,128)(2,1)} copy(bf16[2,64,256]{2,1,0:T(8,128)(2,1)S(1)} %bitcast.6) | data formatting | bytes 131072

commit v5 on v4

--- a/solution.py
+++ b/solution.py
@@ -300,10 +300,7 @@
         for j in range(16):
             summed = summed + shares[:, j : j + 1] * o_recv[b, j].astype(F32)
         g_send[b] = summed.astype(BF16)
-        place = g_full.at[
-            pl.ds(b * HALF, HALF),
-            pl.ds(pl.multiple_of(chip * 128, 128), 128),
-        ]
+        place = g_full.at[b, :, pl.ds(pl.multiple_of(chip * 128, 128), 128)]
         for j, peer in enumerate(chip_peers):
             copy = pltpu.make_async_remote_copy(
                 g_send.at[b],
@@ -319,113 +316,119 @@
         copy.start()
         own_copies.append(copy)
 
-    for copy in own_copies[4:]:
-        copy.wait()
-    swap_copies[0].wait_recv()
-    for copy in g_copies:
-        copy.wait_recv()
-    for side in range(2):
-        attention = nt_dot(g_full[...], out_weight[side]).astype(BF16)
-        for i in range(8):
-            a_send[2 * i + side] = attention[i * 8 : (i + 1) * 8]
-    a_copies = []
-    for j, peer in enumerate(head_peers):
-        copy = pltpu.make_async_remote_copy(
-            a_send.at[peer],
-            a_recv.at[j],
-            a_sems.at[0, j],
-            a_sems.at[1, j],
-            device_id={"head": peer},
-            device_id_type=MESH,
-        )
-        copy.start()
-        a_copies.append(copy)
-    summed = a_send[mine].astype(F32)
-    for j, copy in enumerate(a_copies):
-        copy.wait_recv()
-        summed = summed + a_recv[j].astype(F32)
-    b_send[...] = summed.astype(BF16)
-    b_copies = []
-    for j, peer in enumerate(head_peers):
-        copy = pltpu.make_async_remote_copy(
-            b_send,
-            b_full.at[mine],
-            b_sems.at[0, j],
-            b_sems.at[1, j],
-            device_id={"head": peer},
-            device_id_type=MESH,
-        )
-        copy.start()
-        b_copies.append(copy)
-    b_full[mine] = b_send[...]
+    a_copies, b_copies = [], []
+    for b in range(REQUESTS):
+        own_copies[4 + b].wait()
+        if b == 0:
+            swap_copies[0].wait_recv()
+        for copy in g_copies[b * 7 : (b + 1) * 7]:
+            copy.wait_recv()
+        for side in range(2):
+            attention = nt_dot(g_full[b], out_weight[side])
+            for i in range(8):
+                a_send[b, 2 * i + side] = attention[i * 4 : (i + 1) * 4].astype(BF16)
+        for j, peer in enumerate(head_peers):
+            copy = pltpu.make_async_remote_copy(
+                a_send.at[b, peer],
+                a_recv.at[b, j],
+                a_sems.at[0, b, j],
+                a_sems.at[1, b, j],
+                device_id={"head": peer},
+                device_id_type=MESH,
+            )
+            copy.start()
+            a_copies.append(copy)
+    for b in range(REQUESTS):
+        summed = a_send[b, mine].astype(F32)
+        for j in range(15):
+            a_copies[b * 15 + j].wait_recv()
+            summed = summed + a_recv[b, j].astype(F32)
+        b_send[b] = summed.astype(BF16)
+        for j, peer in enumerate(head_peers):
+            copy = pltpu.make_async_remote_copy(
+                b_send.at[b],
+                b_full.at[b, mine],
+                b_sems.at[0, b, j],
+                b_sems.at[1, b, j],
+                device_id={"head": peer},
+                device_id_type=MESH,
+            )
+            copy.start()
+            b_copies.append(copy)
+        b_full[b, mine] = b_send[b]
+
     for copy in got_residual:
         copy.wait()
     for copy in swap_copies[1:4]:
         copy.wait_recv()
-    for copy in b_copies:
-        copy.wait_recv()
-    squares = jnp.zeros((2 * HALF, 1), F32)
-    scaled = []
-    for side in range(2):
-        attention = jnp.concatenate(
-            [b_full[2 * i + side].astype(F32) for i in range(8)], axis=0
-        )
-        hidden = residual[side].astype(F32) + attention
-        squares = squares + jnp.sum(hidden * hidden, -1, keepdims=True)
-        scaled.append((hidden * gain_rows[side]).astype(BF16))
-
-    s_send[...] = jnp.broadcast_to(jnp.concatenate([squares] * 2, axis=0), (TOKENS, 128)).T[0:1]
-    s_copies = []
-    for j, peer in enumerate(seq_peers):
-        copy = pltpu.make_async_remote_copy(
-            s_send,
-            s_recv.at[j],
-            s_sems.at[0, j],
-            s_sems.at[1, j],
-            device_id={"seq": peer},
-            device_id_type=MESH,
-        )
-        copy.start()
-        s_copies.append(copy)
-    l_copies = []
-    for slot in range(8):
-        swap_copies[4 + slot].wait_recv()
-        part = dot(scaled[0], vocab[0, slot]) + dot(scaled[1], vocab[1, slot])
+    square_parts, l_copies = [], []
+    for b in range(REQUESTS):
+        for copy in b_copies[b * 15 : (b + 1) * 15]:
+            copy.wait_recv()
+        squares = jnp.zeros((HALF, 1), F32)
+        scaled = []
         for side in range(2):
-            l_send[slot, side] = part[:, side * 256 : (side + 1) * 256].astype(BF16)
-        for dk in range(2):
-            j = 2 * slot + dk
-            if slot == 7:
-                if dk == 0:
-                    continue
-                j = 14
-            copy = pltpu.make_async_remote_copy(
-                l_send.at[slot, lax.rem(core + dk, 2)],
-                l_recv.at[j],
-                l_sems.at[0, j],
-                l_sems.at[1, j],
-                device_id={"seq": seq_peers[j]},
-                device_id_type=MESH,
-            )
-            copy.start()
-            l_copies.append(copy)
-    sums = [l_send[7, core].astype(F32), jnp.zeros((2 * HALF, 256), F32)]
+            attention = jnp.concatenate(
+                [b_full[b, 2 * i + side].astype(F32) for i in range(8)], axis=0
+            )
+            hidden = residual[side, b * HALF : (b + 1) * HALF].astype(F32) + attention
+            squares = squares + jnp.sum(hidden * hidden, -1, keepdims=True)
+            scaled.append((hidden * gain_rows[side]).astype(BF16))
+        square_parts.append(squares)
+        if b == 1:
+            squares = jnp.concatenate(square_parts * 2, axis=0)
+            s_send[...] = jnp.broadcast_to(squares, (TOKENS, 128)).T[0:1]
+            s_copies = []
+            for j, peer in enumerate(seq_peers):
+                copy = pltpu.make_async_remote_copy(
+                    s_send,
+                    s_recv.at[j],
+                    s_sems.at[0, j],
+                    s_sems.at[1, j],
+                    device_id={"seq": peer},
+                    device_id_type=MESH,
+                )
+                copy.start()
+                s_copies.append(copy)
+        for slot in range(8):
+            if b == 0:
+                swap_copies[4 + slot].wait_recv()
+            part = dot(scaled[0], vocab[0, slot]) + dot(scaled[1], vocab[1, slot])
+            for side in range(2):
+                l_send[b, slot, side] = part[:, side * 256 : (side + 1) * 256].astype(BF16)
+            for dk in range(2):
+                j = 2 * slot + dk
+                if slot == 7:
+                    if dk == 0:
+                        continue
+                    j = 14
+                copy = pltpu.make_async_remote_copy(
+                    l_send.at[b, slot, lax.rem(core + dk, 2)],
+                    l_recv.at[b, j],
+                    l_sems.at[0, b, j],
+                    l_sems.at[1, b, j],
+                    device_id={"seq": seq_peers[j]},
+                    device_id_type=MESH,
+                )
+                copy.start()
+                l_copies.append(copy)
     squares = [s_send[...], jnp.zeros((1, TOKENS), F32)]
     for j, (_, _, dk) in enumerate(SEQ_STEPS):
         s_copies[j].wait_recv()
         squares[dk] = squares[dk] + s_recv[j]
-    for j, (_, _, dk) in enumerate(SEQ_STEPS):
-        l_copies[j].wait_recv()
-        sums[dk] = sums[dk] + l_recv[j].astype(F32)
-    for dk in range(2):
-        scales = jnp.broadcast_to(
-            lax.rsqrt(squares[dk] / model_width + EPSILON), (128, TOKENS)
-        ).T
-        done = (sums[dk] * scales[: 2 * HALF, 0:1]).astype(BF16)
-        owner = lax.rem(core + dk, 2)
-        for b in range(REQUESTS):
+    scales = [
+        jnp.broadcast_to(lax.rsqrt(total / model_width + EPSILON), (128, TOKENS)).T
+        for total in squares
+    ]
+    for b in range(REQUESTS):
+        sums = [l_send[b, 7, core].astype(F32), jnp.zeros((HALF, 256), F32)]
+        for j, (_, _, dk) in enumerate(SEQ_STEPS):
+            l_copies[b * 15 + j].wait_recv()
+            sums[dk] = sums[dk] + l_recv[b, j].astype(F32)
+        for dk in range(2):
+            owner = lax.rem(core + dk, 2)
             rows = pl.ds(pl.multiple_of(b * DRAFT + owner * HALF, HALF), HALF)
-            logits[rows, :] = done[b * HALF : (b + 1) * HALF]
+            logits[rows, :] = (sums[dk] * scales[dk][b * HALF : (b + 1) * HALF, 0:1]).astype(BF16)
     for copy in o_copies + ml_copies + swap_copies + g_copies + a_copies + b_copies + s_copies + l_copies:
         copy.wait_send()
 
@@ -490,26 +493,26 @@
             pltpu.VMEM((REQUESTS, HEADS, 1, 128), F32),
             pltpu.VMEM((REQUESTS, 16, 1, 128), F32),
             pltpu.VMEM((REQUESTS, 32, 128), BF16),
-            pltpu.VMEM((2 * HALF, 1024), BF16),
-            pltpu.VMEM((16, 8, local_width), BF16),
-            pltpu.VMEM((15, 8, local_width), BF16),
-            pltpu.VMEM((8, local_width), BF16),
-            pltpu.VMEM((16, 8, local_width), BF16),
+            pltpu.VMEM((REQUESTS, HALF, 1024), BF16),
+            pltpu.VMEM((REQUESTS, 16, 4, local_width), BF16),
+            pltpu.VMEM((REQUESTS, 15, 4, local_width), BF16),
+            pltpu.VMEM((REQUESTS, 4, local_width), BF16),
+            pltpu.VMEM((REQUESTS, 16, 4, local_width), BF16),
             pltpu.VMEM((1, TOKENS), F32),
             pltpu.VMEM((15, 1, TOKENS), F32),
-            pltpu.VMEM((8, 2, 2 * HALF, 256), BF16),
-            pltpu.VMEM((15, 2 * HALF, 256), BF16),
+            pltpu.VMEM((REQUESTS, 8, 2, HALF, 256), BF16),
+            pltpu.VMEM((REQUESTS, 15, HALF, 256), BF16),
             dma((16,)),
             dma((8,)),
             dma((REQUESTS, 3)),
             dma((2, REQUESTS, 15)),
             dma((2, REQUESTS, 15)),
             dma((2, REQUESTS, 7)),
-            dma((2, 15)),
-            dma((2, 15)),
+            dma((2, REQUESTS, 15)),
+            dma((2, REQUESTS, 15)),
             dma((2, 15)),
             dma((2, 12)),
-            dma((2, 15)),
+            dma((2, REQUESTS, 15)),
         ],
         compiler_params=pltpu.CompilerParams(
             collective_id=0, has_side_effects=True, vmem_limit_bytes=48 * 1024 * 1024

time: 51.1 us -> 50.9 us (level)
  no operation moved by 1% of the time
where the time goes in v5:
time: 50.9 us; the launch traced here: 50.8 us
  Pallas kernels  50.2 us (99%)
  local copies, waits for them, and re-layouts  0.63 us (1%)
    pallas_call x1, Pallas kernels, per_device(): pl.pallas_call(functools.partial(kernel, model_width), out_shape=jax.Shap...  50.2 us

profile of v5, /device:TPU:1, one launch (start us, length us, event | category | flops | bytes accessed | tf_op | source)
XLA Modules:
  0.0 50.8 jit_solution(8468802580112669970)
XLA Ops:
  0.0 50.2 %shard_map.118 = bf16[128,256]{1,0:T(8,128)(2,1)S(1)} custom-call(s32[2]{0:T(128)} %lengths_hbm.1, s32[2,64]{1,0:T(2,128)} %parents_hbm.1, bf16[2,576,2048]{2,1,0:T(8,128)(2,1)} %bitcast.7, bf16[2,4,576]{2,1,0:T(4,128)(2,1)} %draft_hbm.1, bf16[1024,128]{1,0:T(8,128)(2,1)} %bitcast.9, bf16[1024,64]{1,0:T(8,128)(2,1)} %bitcast.10, ...), custom_call_target="tpu_custom_call" | custom-call | tf_op jit(solution)/shard_map/pallas_call | solution.py:468
  50.2 0.6 %copy.14 = bf16[2,64,256]{2,1,0:T(8,128)(2,1)} copy(bf16[2,64,256]{2,1,0:T(8,128)(2,1)S(1)} %bitcast.6) | data formatting | bytes 131072

commit v6 on v5

--- a/solution.py
+++ b/solution.py
@@ -102,12 +102,6 @@
     chip_peers = seq_peers[0:14:2]
     head_peers = [lax.rem(mine + j, 16) for j in range(1, 16)]
 
-    barrier = pltpu.get_barrier_semaphore()
-    for peer in seq_peers:
-        pl.semaphore_signal(barrier, inc=1, device_id={"seq": peer}, device_id_type=MESH)
-    for peer in head_peers:
-        pl.semaphore_signal(barrier, inc=1, device_id={"head": peer}, device_id_type=MESH)
-
     loads = []
 
     def load(src, dst):
@@ -116,13 +110,16 @@
         copy.start()
         return copy
 
+    got_parents = load(parents_hbm, parents)
+    got_nope = load(nope_hbm, nope)
+    got_key = load(key_hbm, key_weight)
+    got_rope = load(rope_hbm, rope)
+    got_draft = load(draft_hbm, draft)
     got_lengths = load(lengths_hbm, lengths)
-    got_nope = load(nope_hbm, nope)
-    got_rope = load(rope_hbm, rope)
-    got_key = load(key_hbm, key_weight)
-    got_parents = load(parents_hbm, parents)
-    got_draft = load(draft_hbm, draft)
-    got_cache = [load(cache_hbm.at[b], kbuf.at[b]) for b in range(REQUESTS)]
+    got_cache = []
+    for b in range(REQUESTS):
+        parts = [pl.ds(start, WIDTH // 4) for start in range(0, WIDTH, WIDTH // 4)]
+        got_cache.append([load(cache_hbm.at[b, part, :], kbuf.at[b, part, :]) for part in parts])
     got_value = load(value_hbm, value_weight)
     got_out = load(out_hbm, out_weight.at[core])
     got_residual = [
@@ -139,12 +136,19 @@
         owner = lax.div(seat_at(dy, dx, 0), 2)
         columns = pl.ds(pl.multiple_of(owner * 512, 512), 512)
         copy = pltpu.make_async_copy(
-            vocab_hbm.at[:, columns], vocab.at[core, slot], vocab_sems.at[slot]
+            vocab_hbm.at[:, columns], vocab.at[core, :, pl.ds(slot * 512, 512)], vocab_sems.at[slot]
         )
         copy.start()
         got_vocab.append(copy)
 
-    got_parents.wait()
+    barrier = pltpu.get_barrier_semaphore()
+    for peer in seq_peers:
+        pl.semaphore_signal(barrier, inc=1, device_id={"seq": peer}, device_id_type=MESH)
+    for peer in head_peers:
+        pl.semaphore_signal(barrier, inc=1, device_id={"head": peer}, device_id_type=MESH)
+
+    for copy in (got_parents, got_draft, got_nope, got_rope, got_key):
+        copy.wait()
     row = lax.broadcasted_iota(jnp.int32, (DRAFT, DRAFT), 0)
     column = lax.broadcasted_iota(jnp.int32, (DRAFT, DRAFT), 1)
     reaches = [
@@ -163,15 +167,11 @@
             reaches[b], chosen, (((0,), (0,)), ((), ())), preferred_element_type=F32
         )
         tree_bias.append(jnp.where(reached > 0.5, 0.0, NEGATIVE))
-    got_draft.wait()
     dbuf[...] = jnp.zeros((EXTRA, WIDTH), BF16)
     dbuf[0:8, :] = jnp.concatenate([draft[b].astype(F32) for b in range(REQUESTS)], axis=0).astype(BF16)
 
-    got_nope.wait()
     nope32[...] = nope[...].astype(F32)
-    got_rope.wait()
     rope32[...] = rope[...].astype(F32)
-    got_key.wait()
     for h in range(HEADS):
         picked = nope32[pl.ds(h, TOKENS, stride=HEADS), :].astype(BF16)
         absorbed = dot(picked, key_weight[h]).astype(BF16)
@@ -188,7 +188,8 @@
     partner = seq_peers[14]
 
     def score(b):
-        got_cache[b].wait()
+        for copy in got_cache[b]:
+            copy.wait()
         live_bias = jnp.where(position < lengths[b], 0.0, NEGATIVE)
         tree = jnp.concatenate([tree_bias[b]] * HEADS, axis=0)
         return dot(qbuf[b], kbuf[b]) + live_bias, nt_dot(qbuf[b], dbuf[...]) + tree
@@ -261,7 +262,8 @@
         else:
             for slot in range(8):
                 got_vocab[slot].wait()
-                swaps.append((vocab.at[core, slot], vocab.at[core, slot], 4 + slot))
+                place = vocab.at[core, :, pl.ds(slot * 512, 512)]
+                swaps.append((place, place, 4 + slot))
         for src, dst, k in swaps:
             copy = pltpu.make_async_remote_copy(
                 src,
@@ -390,18 +392,18 @@
                 )
                 copy.start()
                 s_copies.append(copy)
+        chips = 4 if b == 0 else 2
         for slot in range(8):
             if b == 0:
                 swap_copies[4 + slot].wait_recv()
-            part = dot(scaled[0], vocab[0, slot]) + dot(scaled[1], vocab[1, slot])
-            for side in range(2):
-                l_send[b, slot, side] = part[:, side * 256 : (side + 1) * 256].astype(BF16)
-            for dk in range(2):
-                j = 2 * slot + dk
-                if slot == 7:
-                    if dk == 0:
-                        continue
-                    j = 14
+        for group in range(0, 8, chips):
+            columns = slice(group * 512, (group + chips) * 512)
+            part = dot(scaled[0], vocab[0, :, columns]) + dot(scaled[1], vocab[1, :, columns])
+            part = part.astype(BF16)
+            for k in range(2 * chips):
+                l_send[b, group + k // 2, k % 2] = part[:, k * 256 : (k + 1) * 256]
+            for j in range(2 * group, min(2 * (group + chips), 15)):
+                slot, dk = (7, 1) if j == 14 else (j // 2, j % 2)
                 copy = pltpu.make_async_remote_copy(
                     l_send.at[b, slot, lax.rem(core + dk, 2)],
                     l_recv.at[b, j],
@@ -484,7 +486,7 @@
             pltpu.VMEM((2, 2 * HALF, local_width), BF16),
             pltpu.VMEM((local_width,), BF16),
             pltpu.VMEM((2, 1, local_width), F32),
-            pltpu.VMEM((2, 8, local_width, 512), BF16),
+            pltpu.VMEM((2, local_width, 4096), BF16),
             pltpu.VMEM((TOKENS * HEADS, 128), F32),
             pltpu.VMEM((TOKENS * HEADS, ROPE), F32),
             pltpu.VMEM((REQUESTS, HEADS * DRAFT, WIDTH), BF16),
@@ -502,7 +504,7 @@
             pltpu.VMEM((15, 1, TOKENS), F32),
             pltpu.VMEM((REQUESTS, 8, 2, HALF, 256), BF16),
             pltpu.VMEM((REQUESTS, 15, HALF, 256), BF16),
-            dma((16,)),
+            dma((20,)),
             dma((8,)),
             dma((REQUESTS, 3)),
             dma((2, REQUESTS, 15)),

time: 50.9 us -> 50.7 us (level)
  no operation moved by 1% of the time
where the time goes in v6:
time: 50.7 us; the launch traced here: 50.6 us
  Pallas kernels  49.9 us (98%)
  local copies, waits for them, and re-layouts  0.63 us (1%)
    pallas_call x1, Pallas kernels, per_device(): pl.pallas_call(functools.partial(kernel, model_width), out_shape=jax.Shap...  49.9 us

profile of v6, /device:TPU:1, one launch (start us, length us, event | category | flops | bytes accessed | tf_op | source)
XLA Modules:
  0.0 50.6 jit_solution(2835566944808150711)
XLA Ops:
  0.0 49.9 %shard_map.118 = bf16[128,256]{1,0:T(8,128)(2,1)S(1)} custom-call(s32[2]{0:T(128)} %lengths_hbm.1, s32[2,64]{1,0:T(2,128)} %parents_hbm.1, bf16[2,576,2048]{2,1,0:T(8,128)(2,1)} %bitcast.7, bf16[2,4,576]{2,1,0:T(4,128)(2,1)} %draft_hbm.1, bf16[1024,128]{1,0:T(8,128)(2,1)} %bitcast.9, bf16[1024,64]{1,0:T(8,128)(2,1)} %bitcast.10, ...), custom_call_target="tpu_custom_call" | custom-call | tf_op jit(solution)/shard_map/pallas_call | solution.py:470
  50.0 0.6 %copy.14 = bf16[2,64,256]{2,1,0:T(8,128)(2,1)} copy(bf16[2,64,256]{2,1,0:T(8,128)(2,1)S(1)} %bitcast.6) | data formatting | bytes 131072

commit v7 on v6

--- a/solution.py
+++ b/solution.py
@@ -19,6 +19,7 @@
 REQUESTS, DRAFT, HEADS, LATENT, ROPE, WIDTH = 2, 64, 8, 512, 64, 576
 TOKENS = REQUESTS * DRAFT
 KEYS, EXTRA = 2048, 128
+KEY_PARTS = [slice(0, KEYS // 2), slice(KEYS // 2, KEYS)]
 HALF = DRAFT // 2
 
 
@@ -116,30 +117,11 @@
     got_rope = load(rope_hbm, rope)
     got_draft = load(draft_hbm, draft)
     got_lengths = load(lengths_hbm, lengths)
-    got_cache = []
-    for b in range(REQUESTS):
+    def load_cache(b):
         parts = [pl.ds(start, WIDTH // 4) for start in range(0, WIDTH, WIDTH // 4)]
-        got_cache.append([load(cache_hbm.at[b, part, :], kbuf.at[b, part, :]) for part in parts])
-    got_value = load(value_hbm, value_weight)
-    got_out = load(out_hbm, out_weight.at[core])
-    got_residual = [
-        load(
-            residual_hbm.at[pl.ds(pl.multiple_of(b * DRAFT + core * HALF, HALF), HALF), :],
-            residual.at[core, pl.ds(b * HALF, HALF), :],
-        )
-        for b in range(REQUESTS)
-    ]
-    got_gain = load(gain_hbm, gain)
-
-    got_vocab = []
-    for slot, (dy, dx) in enumerate(CHIP_STEPS + [(0, 0)]):
-        owner = lax.div(seat_at(dy, dx, 0), 2)
-        columns = pl.ds(pl.multiple_of(owner * 512, 512), 512)
-        copy = pltpu.make_async_copy(
-            vocab_hbm.at[:, columns], vocab.at[core, :, pl.ds(slot * 512, 512)], vocab_sems.at[slot]
-        )
-        copy.start()
-        got_vocab.append(copy)
+        return [load(cache_hbm.at[b, part, :], kbuf.at[b, part, :]) for part in parts]
+
+    got_cache = [load_cache(0)]
 
     barrier = pltpu.get_barrier_semaphore()
     for peer in seq_peers:
@@ -149,6 +131,7 @@
 
     for copy in (got_parents, got_draft, got_nope, got_rope, got_key):
         copy.wait()
+    got_value = load(value_hbm, value_weight)
     row = lax.broadcasted_iota(jnp.int32, (DRAFT, DRAFT), 0)
     column = lax.broadcasted_iota(jnp.int32, (DRAFT, DRAFT), 1)
     reaches = [
@@ -187,28 +170,52 @@
     o_copies, ml_copies, own_copies, swap_copies = [], [], [], []
     partner = seq_peers[14]
 
-    def score(b):
-        for copy in got_cache[b]:
-            copy.wait()
-        live_bias = jnp.where(position < lengths[b], 0.0, NEGATIVE)
+    for copy in got_cache[0] + [got_lengths, got_value]:
+        copy.wait()
+
+    got_cache.append(load_cache(1))
+    got_out = load(out_hbm, out_weight.at[core])
+    got_residual = [
+        load(
+            residual_hbm.at[pl.ds(pl.multiple_of(b * DRAFT + core * HALF, HALF), HALF), :],
+            residual.at[core, pl.ds(b * HALF, HALF), :],
+        )
+        for b in range(REQUESTS)
+    ]
+    got_gain = load(gain_hbm, gain)
+
+    got_vocab = []
+    for slot, (dy, dx) in enumerate(CHIP_STEPS + [(0, 0)]):
+        owner = lax.div(seat_at(dy, dx, 0), 2)
+        columns = pl.ds(pl.multiple_of(owner * 512, 512), 512)
+        copy = pltpu.make_async_copy(
+            vocab_hbm.at[:, columns], vocab.at[core, :, pl.ds(slot * 512, 512)], vocab_sems.at[slot]
+        )
+        copy.start()
+        got_vocab.append(copy)
+
+    for b in range(REQUESTS):
+        if b == 1:
+            for copy in got_cache[1]:
+                copy.wait()
         tree = jnp.concatenate([tree_bias[b]] * HEADS, axis=0)
-        return dot(qbuf[b], kbuf[b]) + live_bias, nt_dot(qbuf[b], dbuf[...]) + tree
-
-    got_lengths.wait()
-    got_value.wait()
-    scores = [score(0), score(1)]
-    for b in range(REQUESTS):
+        drafted = nt_dot(qbuf[b], dbuf[...]) + tree
+        top = jnp.max(drafted, -1, keepdims=True)
+        scores = []
+        for columns in KEY_PARTS:
+            live_bias = jnp.where(position[:, columns] < lengths[b], 0.0, NEGATIVE)
+            scores.append(dot(qbuf[b], kbuf[b, :, columns]) + live_bias)
+            top = jnp.maximum(top, jnp.max(scores[-1], -1, keepdims=True))
+        drafted = jnp.exp2((drafted - top) * scale)
+        total = jnp.sum(drafted, -1, keepdims=True)
+        mixed = dot(drafted.astype(BF16), dbuf[:, 0:LATENT])
+        for columns, cached in zip(KEY_PARTS, scores):
+            cached = jnp.exp2((cached - top) * scale)
+            total = total + jnp.sum(cached, -1, keepdims=True)
+            mixed = mixed + nt_dot(cached.astype(BF16), kbuf[b, 0:LATENT, columns])
+        mixed = mixed.astype(BF16)
         tops = jnp.zeros((DRAFT, 128), F32)
         totals = jnp.zeros((DRAFT, 128), F32)
-        cached, drafted = scores[b]
-        top = jnp.maximum(
-            jnp.max(cached, -1, keepdims=True), jnp.max(drafted, -1, keepdims=True)
-        )
-        cached = jnp.exp2((cached - top) * scale)
-        drafted = jnp.exp2((drafted - top) * scale)
-        total = jnp.sum(cached, -1, keepdims=True) + jnp.sum(drafted, -1, keepdims=True)
-        mixed = nt_dot(cached.astype(BF16), kbuf[b, 0:LATENT, :])
-        mixed = (mixed + dot(drafted.astype(BF16), dbuf[:, 0:LATENT])).astype(BF16)
         for h in range(HEADS):
             sub = slice(h * DRAFT, (h + 1) * DRAFT)
             o_send[b, h] = dot(mixed[sub], value_weight[h]).astype(BF16)
@@ -259,7 +266,6 @@
                         2 + request,
                     )
                 )
-        else:
             for slot in range(8):
                 got_vocab[slot].wait()
                 place = vocab.at[core, :, pl.ds(slot * 512, 512)]

time: 50.7 us -> 50.1 us (0.988)
    pallas_call x1, Pallas kernels: 49.9 us -> 49.4 us  [per_device(): pl.pallas_call(functools.partial(kernel, model_width), out_shape=jax.Shap...]
where the time goes in v7:
time: 50.1 us; the launch traced here: 50 us
  Pallas kernels  49.4 us (99%)
  local copies, waits for them, and re-layouts  0.63 us (1%)
    pallas_call x1, Pallas kernels, per_device(): pl.pallas_call(functools.partial(kernel, model_width), out_shape=jax.Shap...  49.4 us

profile of v7, /device:TPU:1, one launch (start us, length us, event | category | flops | bytes accessed | tf_op | source)
XLA Modules:
  0.0 50.0 jit_solution(4304788871317940777)
XLA Ops:
  0.0 49.4 %shard_map.118 = bf16[128,256]{1,0:T(8,128)(2,1)S(1)} custom-call(s32[2]{0:T(128)} %lengths_hbm.1, s32[2,64]{1,0:T(2,128)} %parents_hbm.1, bf16[2,576,2048]{2,1,0:T(8,128)(2,1)} %bitcast.7, bf16[2,4,576]{2,1,0:T(4,128)(2,1)} %draft_hbm.1, bf16[1024,128]{1,0:T(8,128)(2,1)} %bitcast.9, bf16[1024,64]{1,0:T(8,128)(2,1)} %bitcast.10, ...), custom_call_target="tpu_custom_call" | custom-call | tf_op jit(solution)/shard_map/pallas_call | solution.py:476
  49.4 0.6 %copy.14 = bf16[2,64,256]{2,1,0:T(8,128)(2,1)} copy(bf16[2,64,256]{2,1,0:T(8,128)(2,1)S(1)} %bitcast.6) | data formatting | bytes 131072

commit v8 on v7

--- a/solution.py
+++ b/solution.py
@@ -51,6 +51,7 @@
     kbuf,
     draft,
     dbuf,
+    tree_bias,
     nope,
     rope,
     key_weight,
@@ -142,14 +143,13 @@
         reaches = [jnp.where(dot(r, r) > 0.5, 1.0, 0.0).astype(BF16) for r in reaches]
     row = lax.broadcasted_iota(jnp.int32, (DRAFT, EXTRA), 0)
     column = lax.broadcasted_iota(jnp.int32, (DRAFT, EXTRA), 1)
-    tree_bias = []
     for b in range(REQUESTS):
         chosen = (column >= 4 * b) & (column < 4 * b + 4) & (row == seat * 4 + column - 4 * b)
         chosen = jnp.where(chosen, 1.0, 0.0).astype(BF16)
         reached = lax.dot_general(
             reaches[b], chosen, (((0,), (0,)), ((), ())), preferred_element_type=F32
         )
-        tree_bias.append(jnp.where(reached > 0.5, 0.0, NEGATIVE))
+        tree_bias[b] = jnp.where(reached > 0.5, 0.0, NEGATIVE)
     dbuf[...] = jnp.zeros((EXTRA, WIDTH), BF16)
     dbuf[0:8, :] = jnp.concatenate([draft[b].astype(F32) for b in range(REQUESTS)], axis=0).astype(BF16)
 
@@ -167,7 +167,6 @@
     scale = math.log2(math.e) / math.sqrt(192.0)
     lane = lax.broadcasted_iota(jnp.int32, (DRAFT, 128), 1)
     position = seat * KEYS + lax.broadcasted_iota(jnp.int32, (1, KEYS), 1)
-    o_copies, ml_copies, own_copies, swap_copies = [], [], [], []
     partner = seq_peers[14]
 
     for copy in got_cache[0] + [got_lengths, got_value]:
@@ -194,10 +193,71 @@
         copy.start()
         got_vocab.append(copy)
 
-    for b in range(REQUESTS):
-        if b == 1:
+    def o_copy(b, j):
+        peer = seq_peers[j]
+        half = pl.ds(pl.multiple_of(lax.rem(peer, 2) * HALF, HALF), HALF)
+        return pltpu.make_async_remote_copy(
+            o_send.at[b, lax.div(peer, 2), half, :],
+            o_recv.at[b, j],
+            o_sems.at[0, b, j],
+            o_sems.at[1, b, j],
+            device_id={"seq": peer},
+            device_id_type=MESH,
+        )
+
+    def ml_copy(b, j):
+        peer = seq_peers[j]
+        return pltpu.make_async_remote_copy(
+            ml_send.at[b, lax.div(peer, 2)],
+            ml_recv.at[b, j],
+            ml_sems.at[0, b, j],
+            ml_sems.at[1, b, j],
+            device_id={"seq": peer},
+            device_id_type=MESH,
+        )
+
+    def own_copy(b, k):
+        half = pl.ds(pl.multiple_of(core * HALF, HALF), HALF)
+        src, dst = (
+            (o_send.at[b, chip, half, :], o_recv.at[b, 15]),
+            (ml_send.at[b, chip], ml_recv.at[b, 15]),
+        )[k]
+        return pltpu.make_async_copy(src, dst, local_sems.at[b, k])
+
+    swaps = [
+        (out_weight.at[core], out_weight.at[core]),
+        (gain_rows.at[core], gain_rows.at[core]),
+    ]
+    for request in range(REQUESTS):
+        other_rows = pl.multiple_of(request * DRAFT + (1 - core) * HALF, HALF)
+        swaps.append(
+            (
+                residual_hbm.at[pl.ds(other_rows, HALF), :],
+                residual.at[core, pl.ds(request * HALF, HALF), :],
+            )
+        )
+    for slot in range(8):
+        place = vocab.at[core, :, pl.ds(slot * 512, 512)]
+        swaps.append((place, place))
+    swap_copies = [
+        pltpu.make_async_remote_copy(
+            src,
+            dst,
+            swap_sems.at[0, k],
+            swap_sems.at[1, k],
+            device_id={"seq": partner},
+            device_id_type=MESH,
+        )
+        for k, (src, dst) in enumerate(swaps)
+    ]
+
+    @pl.loop(0, REQUESTS)
+    def _(b):
+        @pl.when(b == 1)
+        def _():
             for copy in got_cache[1]:
                 copy.wait()
+
         tree = jnp.concatenate([tree_bias[b]] * HEADS, axis=0)
         drafted = nt_dot(qbuf[b], dbuf[...]) + tree
         top = jnp.max(drafted, -1, keepdims=True)
@@ -224,70 +284,30 @@
         turned = jnp.concatenate([tops, totals], axis=0).T
         for h in range(HEADS):
             ml_send[b, h] = turned[h : h + 1]
-        if b == 0:
+
+        @pl.when(b == 0)
+        def _():
             pl.semaphore_wait(barrier, 30)
-        for j, step in enumerate(SEQ_STEPS):
-            peer = seq_peers[j]
-            there, their_core = lax.div(peer, 2), lax.rem(peer, 2)
-            half = pl.ds(pl.multiple_of(their_core * 32, 32), 32)
-            copy = pltpu.make_async_remote_copy(
-                o_send.at[b, there, half, :],
-                o_recv.at[b, j],
-                o_sems.at[0, b, j],
-                o_sems.at[1, b, j],
-                device_id={"seq": peer},
-                device_id_type=MESH,
-            )
-            copy.start()
-            o_copies.append(copy)
-            copy = pltpu.make_async_remote_copy(
-                ml_send.at[b, there],
-                ml_recv.at[b, j],
-                ml_sems.at[0, b, j],
-                ml_sems.at[1, b, j],
-                device_id={"seq": peer},
-                device_id_type=MESH,
-            )
-            copy.start()
-            ml_copies.append(copy)
-        swaps = []
-        if b == 0:
+
+        for j in range(15):
+            o_copy(b, j).start()
+            ml_copy(b, j).start()
+        for k in range(2):
+            own_copy(b, k).start()
+
+        @pl.when(b == 0)
+        def _():
             got_out.wait()
             got_gain.wait()
             gain_rows[core] = gain[...].astype(F32)[None, :]
-            swaps.append((out_weight.at[core], out_weight.at[core], 0))
-            swaps.append((gain_rows.at[core], gain_rows.at[core], 1))
-            for request in range(REQUESTS):
-                other_rows = pl.multiple_of(request * DRAFT + (1 - core) * HALF, HALF)
-                swaps.append(
-                    (
-                        residual_hbm.at[pl.ds(other_rows, HALF), :],
-                        residual.at[core, pl.ds(request * HALF, HALF), :],
-                        2 + request,
-                    )
-                )
-            for slot in range(8):
-                got_vocab[slot].wait()
-                place = vocab.at[core, :, pl.ds(slot * 512, 512)]
-                swaps.append((place, place, 4 + slot))
-        for src, dst, k in swaps:
-            copy = pltpu.make_async_remote_copy(
-                src,
-                dst,
-                swap_sems.at[0, k],
-                swap_sems.at[1, k],
-                device_id={"seq": partner},
-                device_id_type=MESH,
-            )
-            copy.start()
-            swap_copies.append(copy)
-        half = pl.ds(pl.multiple_of(core * 32, 32), 32)
-        for k, (src, dst) in enumerate(
-            ((o_send.at[b, chip, half, :], o_recv.at[b, 15]), (ml_send.at[b, chip], ml_recv.at[b, 15]))
-        ):
-            copy = pltpu.make_async_copy(src, dst, local_sems.at[b, k])
-            copy.start()
-            own_copies.append(copy)
+            for copy in got_vocab:
+                copy.wait()
+            for copy in swap_copies:
+                copy.start()
+
+    o_copies = [o_copy(b, j) for b in range(REQUESTS) for j in range(15)]
+    ml_copies = [ml_copy(b, j) for b in range(REQUESTS) for j in range(15)]
+    own_copies = [own_copy(b, k) for b in range(REQUESTS) for k in range(2)]
 
     g_copies = []
     for b in range(REQUESTS):
@@ -484,6 +504,7 @@
             pltpu.VMEM((REQUESTS, WIDTH, KEYS), BF16),
             pltpu.VMEM((REQUESTS, 4, WIDTH), BF16),
             pltpu.VMEM((EXTRA, WIDTH), BF16),
+            pltpu.VMEM((REQUESTS, DRAFT, EXTRA), F32),
             pltpu.VMEM((TOKENS * HEADS, 128), BF16),
             pltpu.VMEM((TOKENS * HEADS, ROPE), BF16),
             pltpu.VMEM((HEADS, 128, LATENT), BF16),

time: 50.1 us -> 50.2 us (level)
  no operation moved by 1% of the time
where the time goes in v8:
time: 50.2 us; the launch traced here: 50.1 us
  Pallas kernels  49.5 us (99%)
  local copies, waits for them, and re-layouts  0.63 us (1%)
    pallas_call x1, Pallas kernels, per_device(): pl.pallas_call(functools.partial(kernel, model_width), out_shape=jax.Shap...  49.5 us

profile of v8, /device:TPU:1, one launch (start us, length us, event | category | flops | bytes accessed | tf_op | source)
XLA Modules:
  0.0 50.1 jit_solution(3380252311708288719)
XLA Ops:
  0.0 49.5 %shard_map.118 = bf16[128,256]{1,0:T(8,128)(2,1)S(1)} custom-call(s32[2]{0:T(128)} %lengths_hbm.1, s32[2,64]{1,0:T(2,128)} %parents_hbm.1, bf16[2,576,2048]{2,1,0:T(8,128)(2,1)} %bitcast.7, bf16[2,4,576]{2,1,0:T(4,128)(2,1)} %draft_hbm.1, bf16[1024,128]{1,0:T(8,128)(2,1)} %bitcast.9, bf16[1024,64]{1,0:T(8,128)(2,1)} %bitcast.10, ...), custom_call_target="tpu_custom_call" | custom-call | tf_op jit(solution)/shard_map/pallas_call | solution.py:496
  49.5 0.6 %copy.14 = bf16[2,64,256]{2,1,0:T(8,128)(2,1)} copy(bf16[2,64,256]{2,1,0:T(8,128)(2,1)S(1)} %bitcast.6) | data formatting | bytes 131072

commit v9 on v8

--- a/solution.py
+++ b/solution.py
@@ -16,6 +16,7 @@
 
 CHIP_STEPS = [(2, 1), (1, 1), (3, 1), (2, 0), (0, 1), (1, 0), (3, 0)]
 SEQ_STEPS = [(dy, dx, dk) for dy, dx in CHIP_STEPS for dk in (0, 1)] + [(0, 0, 1)]
+HEAD_STEPS = [(dx, dz) for dz in (4, 3, 5, 2, 6, 1, 7) for dx in (1, 0)] + [(1, 0)]
 REQUESTS, DRAFT, HEADS, LATENT, ROPE, WIDTH = 2, 64, 8, 512, 64, 576
 TOKENS = REQUESTS * DRAFT
 KEYS, EXTRA = 2048, 128
@@ -102,7 +103,10 @@
 
     seq_peers = [seat_at(*step) for step in SEQ_STEPS]
     chip_peers = seq_peers[0:14:2]
-    head_peers = [lax.rem(mine + j, 16) for j in range(1, 16)]
+    head_peers = [
+        lax.rem(lax.div(mine, 8) + dx, 2) * 8 + lax.rem(lax.rem(mine, 8) + dz, 8)
+        for dx, dz in HEAD_STEPS
+    ]
 
     loads = []
 
@@ -403,21 +407,6 @@
             squares = squares + jnp.sum(hidden * hidden, -1, keepdims=True)
             scaled.append((hidden * gain_rows[side]).astype(BF16))
         square_parts.append(squares)
-        if b == 1:
-            squares = jnp.concatenate(square_parts * 2, axis=0)
-            s_send[...] = jnp.broadcast_to(squares, (TOKENS, 128)).T[0:1]
-            s_copies = []
-            for j, peer in enumerate(seq_peers):
-                copy = pltpu.make_async_remote_copy(
-                    s_send,
-                    s_recv.at[j],
-                    s_sems.at[0, j],
-                    s_sems.at[1, j],
-                    device_id={"seq": peer},
-                    device_id_type=MESH,
-                )
-                copy.start()
-                s_copies.append(copy)
         chips = 4 if b == 0 else 2
         for slot in range(8):
             if b == 0:
@@ -440,6 +429,21 @@
                 )
                 copy.start()
                 l_copies.append(copy)
+            if b == 1 and group == 0:
+                squares = jnp.concatenate(square_parts * 2, axis=0)
+                s_send[...] = jnp.broadcast_to(squares, (TOKENS, 128)).T[0:1]
+                s_copies = []
+                for j, peer in enumerate(seq_peers):
+                    copy = pltpu.make_async_remote_copy(
+                        s_send,
+                        s_recv.at[j],
+                        s_sems.at[0, j],
+                        s_sems.at[1, j],
+                        device_id={"seq": peer},
+                        device_id_type=MESH,
+                    )
+                    copy.start()
+                    s_copies.append(copy)
     squares = [s_send[...], jnp.zeros((1, TOKENS), F32)]
     for j, (_, _, dk) in enumerate(SEQ_STEPS):
         s_copies[j].wait_recv()

time: 50.2 us -> 50 us (level)
  no operation moved by 1% of the time
where the time goes in v9:
time: 50 us
  Pallas kernels  49.3 us (99%)
  local copies, waits for them, and re-layouts  0.63 us (1%)
    pallas_call x1, Pallas kernels, per_device(): pl.pallas_call(functools.partial(kernel, model_width), out_shape=jax.Shap...  49.3 us

profile of v9, /device:TPU:1, one launch (start us, length us, event | category | flops | bytes accessed | tf_op | source)
XLA Modules:
  0.0 50.0 jit_solution(4275791793965589122)
XLA Ops:
  0.0 49.3 %shard_map.118 = bf16[128,256]{1,0:T(8,128)(2,1)S(1)} custom-call(s32[2]{0:T(128)} %lengths_hbm.1, s32[2,64]{1,0:T(2,128)} %parents_hbm.1, bf16[2,576,2048]{2,1,0:T(8,128)(2,1)} %bitcast.7, bf16[2,4,576]{2,1,0:T(4,128)(2,1)} %draft_hbm.1, bf16[1024,128]{1,0:T(8,128)(2,1)} %bitcast.9, bf16[1024,64]{1,0:T(8,128)(2,1)} %bitcast.10, ...), custom_call_target="tpu_custom_call" | custom-call | tf_op jit(solution)/shard_map/pallas_call | solution.py:500
  49.3 0.6 %copy.14 = bf16[2,64,256]{2,1,0:T(8,128)(2,1)} copy(bf16[2,64,256]{2,1,0:T(8,128)(2,1)S(1)} %bitcast.6) | data formatting | bytes 131072

commit v10 on v8

--- a/solution.py
+++ b/solution.py
@@ -418,7 +418,7 @@
                 )
                 copy.start()
                 s_copies.append(copy)
-        chips = 4 if b == 0 else 2
+        chips = 4
         for slot in range(8):
             if b == 0:
                 swap_copies[4 + slot].wait_recv()

time: 50.2 us -> 50.5 us (level)
  no operation moved by 1% of the time
where the time goes in v10:
time: 50.5 us; the launch traced here: 50.4 us
  Pallas kernels  49.8 us (99%)
  local copies, waits for them, and re-layouts  0.63 us (1%)
    pallas_call x1, Pallas kernels, per_device(): pl.pallas_call(functools.partial(kernel, model_width), out_shape=jax.Shap...  49.8 us

profile of v10, /device:TPU:1, one launch (start us, length us, event | category | flops | bytes accessed | tf_op | source)
XLA Modules:
  0.0 50.4 jit_solution(15494989326492866723)
XLA Ops:
  0.0 49.8 %shard_map.118 = bf16[128,256]{1,0:T(8,128)(2,1)S(1)} custom-call(s32[2]{0:T(128)} %lengths_hbm.1, s32[2,64]{1,0:T(2,128)} %parents_hbm.1, bf16[2,576,2048]{2,1,0:T(8,128)(2,1)} %bitcast.7, bf16[2,4,576]{2,1,0:T(4,128)(2,1)} %draft_hbm.1, bf16[1024,128]{1,0:T(8,128)(2,1)} %bitcast.9, bf16[1024,64]{1,0:T(8,128)(2,1)} %bitcast.10, ...), custom_call_target="tpu_custom_call" | custom-call | tf_op jit(solution)/shard_map/pallas_call | solution.py:496
  49.8 0.6 %copy.14 = bf16[2,64,256]{2,1,0:T(8,128)(2,1)} copy(bf16[2,64,256]{2,1,0:T(8,128)(2,1)S(1)} %bitcast.6) | data formatting | bytes 131072
